TPU v7x, 128 devices: a whole 4x4x4 slice. The times are simulated.
128 devices in a mesh: pole: 8 (over x_lo, z), row: 4 (over x_hi, core), col: 4 (over y).
Axes of the slice: x: 4 (x_hi: 2, x_lo: 2; x = x_hi * 2 + x_lo), y: 4, z: 4, core: 2. Of those that a mesh axis runs over, the one named last changes fastest.
Arguments:
- inverse_tile: float32 [8, 2, 4608, 4608], P('pole', None, 'row', 'col'), may hold values from -0.0625 to 0.0625
- lower_factor: float32 [8, 2, 256, 4608], P('pole', None, 'row', 'col'), may hold values from -6 to 6
- upper_factor: float32 [8, 2, 256, 4608], P('pole', None, 'col', 'row'), may hold values from -1.5 to 1.5
- pivot_inverse: float32 [8, 2, 256, 256], P('pole', None, 'row', 'col'), may hold values from -48 to 48
- pole_weights: float32 [8, 2], P('pole'), may hold values from -3 to 3
- block_owners: int32 [2304, 6], replicated, may hold values from 0 to 127, all different within a row; in each aligned block of 18 rows (0 to 17, 18 to 35, ...) at most 2 rows name the same one
- basis_ancestor: float32 [4608, 16384], P(None, ('pole', 'row', 'col')), may hold values from -3 to 3
- basis_super: float32 [256, 16384], P(None, ('pole', 'row', 'col')), may hold values from -0.09375 to 0.09375
Outputs:
- upper_density: float32 [256, 4608], P(('pole', 'row'), 'col')
- charge: float32 [16384], P(('pole', 'row', 'col'))
Inputs may be any that keep to these rules, and one draw needn't show every extreme that they name: `block_owners`: each row names 6 different owners. Among the rows k * 18 to (k + 1) * 18 - 1, for each k, no owner is named more than 2 times, and in every draw some owner is named exactly 2 times there. Every owner is named by some row.
All inputs are finite; a program needn't handle non-finite values.
Results may differ from a plain program's by a relative error of at most 0.0003.
Values sent between devices are 32-bit elements; how exact they have to be, the bound alone decides.
A program may use at most 64 MiB of HBM per device.

v0:
```python
import jax
import jax.numpy as jnp
from jax import lax
from jax.sharding import PartitionSpec as P

NB = 18
TOPK = 6


def contract_last(left, right):
    return lax.dot_general(
        left,
        right,
        (((1,), (1,)), ((), ())),
        precision=lax.Precision.HIGHEST,
        preferred_element_type=jnp.float32,
    )


def matmul(left, right):
    return jnp.dot(left, right, precision=lax.Precision.HIGHEST, preferred_element_type=jnp.float32)


def body(
    inverse_tile,
    lower_factor,
    upper_factor,
    pivot_inverse,
    pole_weights,
    block_owners,
    basis_ancestor,
    basis_super,
):
    tile_re = inverse_tile[0, 0]
    tile_im = inverse_tile[0, 1]
    weight_re = pole_weights[0, 0]
    weight_im = pole_weights[0, 1]
    tile_cols = tile_re.shape[1]
    super_width = basis_super.shape[0]
    fragment = lax.all_gather(lower_factor, "row", axis=2, tiled=True)
    frag_re = fragment[0, 0]
    frag_im = fragment[0, 1]
    prod_re = contract_last(tile_re, frag_re) - contract_last(tile_im, frag_im)
    prod_im = contract_last(tile_re, frag_im) + contract_last(tile_im, frag_re)
    tile_lower = jnp.stack([prod_re, prod_im])
    lower_re = tile_lower[0]
    lower_im = tile_lower[1]
    fragment = lax.all_gather(upper_factor, "col", axis=2, tiled=True)
    frag_re = fragment[0, 0]
    frag_im = fragment[0, 1]
    first_re = matmul(frag_re, tile_re) - matmul(frag_im, tile_im)
    first_im = matmul(frag_re, tile_im) + matmul(frag_im, tile_re)
    second_re = matmul(frag_re, lower_re) - matmul(frag_im, lower_im)
    second_im = matmul(frag_re, lower_im) + matmul(frag_im, lower_re)
    upper_all = jnp.stack(
        [jnp.concatenate([first_re, second_re], 1), jnp.concatenate([first_im, second_im], 1)]
    )
    lower_term = -(weight_re * lower_im + weight_im * lower_re)
    upper_term = -(
        weight_re * upper_all[1, :, :tile_cols] + weight_im * upper_all[0, :, :tile_cols]
    )
    pivot_term = weight_re * upper_all[1, :, tile_cols:] + weight_im * upper_all[0, :, tile_cols:]
    piece_rows = pivot_inverse.shape[2]
    piece_cols = pivot_inverse.shape[3]
    pivot_piece = weight_re * pivot_inverse[0, 1] + weight_im * pivot_inverse[0, 0]
    placed = lax.dynamic_update_slice(
        jnp.zeros_like(pivot_term),
        pivot_piece,
        (lax.axis_index("row") * piece_rows, lax.axis_index("col") * piece_cols),
    )
    pivot_term = pivot_term + placed
    lower_rows = lax.psum_scatter(lower_term, ("pole", "col"), scatter_dimension=0, tiled=True)
    upper_density = lax.psum_scatter(upper_term, ("pole", "row"), scatter_dimension=0, tiled=True)
    pivot_density = lax.psum(pivot_term, ("pole", "row", "col"))
    n_pole = lax.axis_size("pole")
    n_row = lax.axis_size("row")
    n_col = lax.axis_size("col")
    devices_all = n_pole * n_row * n_col
    capacity = max(2, (NB * TOPK + devices_all - 1) // devices_all)
    rows_here = lower_rows.shape[0]
    block_rows = rows_here // NB
    position = (
        lax.axis_index("row") * (n_pole * n_col)
        + lax.axis_index("pole") * n_col
        + lax.axis_index("col")
    )
    first_block = position * NB
    owners_here = lax.dynamic_slice_in_dim(block_owners, first_block, NB, 0)
    flat_owner = owners_here.reshape(-1)
    one_hot = (flat_owner[:, None] == jnp.arange(devices_all, dtype=jnp.int32)[None, :]).astype(
        jnp.int32
    )
    earlier = jnp.cumsum(one_hot, 0) - one_hot
    slot_rank = jnp.sum(earlier * one_hot, 1)
    slot_index = (flat_owner * capacity + slot_rank).reshape(NB, TOPK)
    selector = jnp.sum(
        (
            slot_index[:, :, None]
            == jnp.arange(devices_all * capacity, dtype=jnp.int32)[None, None, :]
        ).astype(jnp.int32),
        1,
    )
    block_values = lower_rows.reshape(NB, block_rows * super_width)
    send_values = lax.dot_general(
        selector.astype(jnp.float32),
        block_values,
        (((0,), (0,)), ((), ())),
        precision=lax.Precision.HIGHEST,
        preferred_element_type=jnp.float32,
    )
    block_ids = first_block + jnp.arange(NB, dtype=jnp.int32)
    send_ids = jnp.sum(selector * block_ids[:, None], 0)
    recv_values, recv_ids = (
        lax.all_to_all(
            send_values.reshape(devices_all, capacity, block_rows * super_width),
            ("pole", "row", "col"),
            split_axis=0,
            concat_axis=0,
            tiled=True,
        ),
        lax.all_to_all(
            send_ids.reshape(devices_all, capacity),
            ("pole", "row", "col"),
            split_axis=0,
            concat_axis=0,
            tiled=True,
        ),
    )
    row_ids = (
        recv_ids.reshape(-1)[:, None] * block_rows
        + jnp.arange(block_rows, dtype=jnp.int32)[None, :]
    ).reshape(-1)
    ancestor_rows = jnp.take(basis_ancestor, row_ids, axis=0)
    received = recv_values.reshape(-1, super_width)
    projected = matmul(received, basis_super)
    ancestor_part = jnp.sum(ancestor_rows * projected, 0)
    pivot_part = jnp.sum(basis_super * matmul(pivot_density, basis_super), 0)
    charge = ancestor_part + pivot_part
    return (upper_density, charge)


def solution(mesh):
    placed = (
        P("pole", None, "row", "col"),
        P("pole", None, "row", "col"),
        P("pole", None, "col", "row"),
        P("pole", None, "row", "col"),
        P("pole", None),
        P(),
        P(None, ("pole", "row", "col")),
        P(None, ("pole", "row", "col")),
    )
    return jax.shard_map(
        body,
        mesh=mesh,
        in_specs=placed,
        out_specs=(P(("pole", "row"), "col"), P(("pole", "row", "col"))),
        check_vma=False,
    )
```

profile of v0, /device:TPU:0, one launch (start us, length us, event | category | flops | bytes accessed | tf_op | source)
XLA Modules:
  0.0 472.9 jit_solution(9224884598857572701)
XLA Ops:
  10.4 11.2 %all-to-all-start = ((s32[128,1,2]{2,1,0:T(1,128)}), s32[128,1,2]{2,1,0:T(1,128)S(1)}, u32[]{:S(2)}, u32[]{:S(2)}) async-start(s32[128,1,2]{2,1,0:T(1,128)} %bitcast.13), calls=%async_computation | async-start | bytes 131072 | tf_op jit(solution)/shard_map/all_to_all | solution.py:121
  26.5 4.1 all-to-all-done
  31.4 8.9 %all-gather.5.cloned.1.call-done = f32[1,2,256,1152]{3,2,1,0:T(8,128)} async-done(((f32[1,2,64,1152]{3,2,1,0:T(8,128)}), f32[1,2,256,1152]{3,2,1,0:T(8,128)}) %all-gather.5.cloned.1.call-update) | async-done | bytes 2359312 | tf_op jit(solution)/shard_map/all_gather | solution.py:40
  40.3 7.3 %fusion.5 = f32[1152,256]{1,0:T(8,128)S(1)} fusion(f32[1,2,1152,1152]{3,2,1,0:T(8,128)} %param.8, f32[1,2,256,1152]{3,2,1,0:T(8,128)} %all-gather.5.cloned.1.call-done), kind=kOutput, calls=%fused_computation.5 | convolution fusion | flops 4076863488 | bytes 7667712 | tf_op jit(solution)/shard_map/dot_general | solution.py:11
  47.6 7.6 %fusion.3 = f32[1152,256]{1,0:T(8,128)S(1)} fusion(f32[1,2,1152,1152]{3,2,1,0:T(8,128)} %param.8, f32[1,2,256,1152]{3,2,1,0:T(8,128)} %all-gather.5.cloned.1.call-done), kind=kOutput, calls=%fused_computation.3 | convolution fusion | flops 4076863488 | bytes 7667712 | tf_op jit(solution)/shard_map/dot_general | solution.py:11
  55.3 4.8 %fusion.28 = f32[1152,256]{1,0:T(8,128)S(1)} fusion(f32[1152,256]{1,0:T(8,128)S(1)} %fusion.5, f32[1,2,1152,1152]{3,2,1,0:T(8,128)S(1)} %copy-done.1, f32[1,2,256,1152]{3,2,1,0:T(8,128)S(1)} %copy-done.4), kind=kOutput, calls=%fused_computation.26 | convolution fusion | flops 4077158400 | bytes 8847360 | tf_op jit(solution)/shard_map/dot_general | solution.py:11
  60.1 7.6 %add_negate_fusion = (f32[1152,256]{1,0:T(8,128)}, f32[1152,256]{1,0:T(8,128)}) fusion(f32[1152,256]{1,0:T(8,128)S(1)} %fusion.28, f32[]{:T(128)} %bitcast.9, f32[]{:T(128)} %bitcast, f32[1152,256]{1,0:T(8,128)S(1)} %fusion.3, f32[1,2,256,1152]{3,2,1,0:T(8,128)S(1)} %copy-done.4, f32[1,2,1152,1152]{3,2,1,0:T(8,128)S(1)} %copy-done.1), kind=kOutput, calls=%fused_computation.40 | convolution fusion | flops 4078338048 | bytes 11206664 | tf_op jit(solution)/shard_map/dot_general | solution.py:11
  67.7 91.4 %fusion = f32[40,256]{1,0:T(8,128)} fusion(f32[1152,256]{1,0:T(8,128)} %get-tuple-element.6), kind=kCustom, calls=%all-reduce-scatter | all-reduce-scatter fusion | flops 327681 | bytes 1221120
  159.1 1.9 collective-permute-start
  161.0 1.9 collective-permute-start.1
  162.9 1.9 collective-permute-start.2
  165.5 1.4 collective-permute-start.3
  167.0 2.7 fusion.45
  169.7 8.1 %fusion.7 = f32[256,1152]{1,0:T(8,128)S(1)} fusion(f32[1,2,1152,1152]{3,2,1,0:T(8,128)} %param.8, f32[1,2,256,1152]{3,2,1,0:T(8,128)S(1)} %copy-done.2), kind=kOutput, calls=%fused_computation.7 | convolution fusion | flops 4076863488 | bytes 7667712 | tf_op jit(solution)/shard_map/dot_general | solution.py:21
  177.9 8.1 %fusion.1 = f32[256,1152]{1,0:T(8,128)S(1)} fusion(f32[1,2,1152,1152]{3,2,1,0:T(8,128)} %param.8, f32[1,2,256,1152]{3,2,1,0:T(8,128)S(1)} %copy-done.2), kind=kOutput, calls=%fused_computation.1 | convolution fusion | flops 4076863488 | bytes 7667712 | tf_op jit(solution)/shard_map/dot_general | solution.py:21
  186.0 1.5 fusion.44
  187.5 1.3 fusion.40
  188.8 1.3 fusion.41
  190.2 5.5 %fusion.25 = f32[256,1152]{1,0:T(8,128)S(1)} fusion(f32[256,1152]{1,0:T(8,128)S(1)} %fusion.7, f32[1,2,1152,1152]{3,2,1,0:T(8,128)S(1)} %bitcast.86, f32[1,2,256,1152]{3,2,1,0:T(8,128)S(1)} %copy-done.2), kind=kOutput, calls=%fused_computation.25 | convolution fusion | flops 4077158400 | bytes 8847360 | tf_op jit(solution)/shard_map/dot_general | solution.py:21
  195.7 5.8 %fusion.34 = f32[256,1152]{1,0:T(8,128)S(1)} fusion(f32[256,1152]{1,0:T(8,128)S(1)} %fusion.1, f32[1,2,1152,1152]{3,2,1,0:T(8,128)S(1)} %bitcast.86, f32[1,2,256,1152]{3,2,1,0:T(8,128)S(1)} %copy-done.2), kind=kOutput, calls=%fused_computation.28 | convolution fusion | flops 4077158400 | bytes 8847360 | tf_op jit(solution)/shard_map/dot_general | solution.py:21
  202.8 1.3 fusion.46
  204.2 1.4 bitcast_add_fusion
  207.5 2.6 concatenate.8
  210.7 1.2 copy.38
  211.9 13.3 %all-to-all-start.1 = ((f32[128,2,512]{2,1,0:T(2,128)}), f32[128,2,512]{2,1,0:T(2,128)S(1)}, u32[]{:S(2)}, u32[]{:S(2)}) async-start(f32[128,2,512]{2,1,0:T(2,128)} %copy.38), calls=%async_computation.1 | async-start | bytes 1048576 | tf_op jit(solution)/shard_map/all_to_all | solution.py:114
  225.2 4.1 fusion.39
  229.4 1.6 gather_fusion
  231.1 127.6 %all-reduce.6.cloned.1.call-done = f32[256,256]{1,0:T(8,128)} async-done(((f32[256,256]{1,0:T(8,128)}), f32[256,256]{1,0:T(8,128)}) %all-reduce.6.cloned.1.call-update) | async-done | bytes 262160 | tf_op jit(solution)/shard_map/psum | solution.py:74
  358.7 1.3 fusion.43
  360.5 1.5 fusion.42
  362.5 102.0 %all-reduce.8.cloned.1.call-done = f32[256,1152]{1,0:T(8,128)} async-done(((f32[256,1152]{1,0:T(8,128)}), f32[256,1152]{1,0:T(8,128)}) %all-reduce.8.cloned.1.call-update) | async-done | bytes 1179664
  464.5 1.4 constant_dynamic-slice_fusion.1
  (83 shorter events, 12.8 us)
Async XLA Ops:
  7.2 222.2 %copy-start = (f32[4608,128]{1,0:T(8,128)S(1)}, f32[4608,128]{1,0:T(8,128)}, u32[]{:S(2)}) copy-start(f32[4608,128]{1,0:T(8,128)} %param.14) | copy-start | bytes 7077892
  7.2 16.6 %copy-start.13 = (u32[128]{0:T(128)S(1)}, u32[128]{0:T(128)}, u32[]{:S(2)}) copy-start(u32[128]{0:T(128)} %constant.64) | copy-start | bytes 1540
  7.2 18.0 %copy-start.14 = (u32[128]{0:T(128)S(1)}, u32[128]{0:T(128)}, u32[]{:S(2)}) copy-start(u32[128]{0:T(128)} %constant.60) | copy-start | bytes 1540
  7.2 15.2 %copy-start.12 = (f32[1,2]{1,0:T(1,128)S(1)}, f32[1,2]{1,0:T(1,128)}, u32[]{:S(2)}) copy-start(f32[1,2]{1,0:T(1,128)} %param.12) | copy-start | bytes 28
  7.2 33.1 %all-gather.5.cloned.1.call-start = ((), (), s32[]{:S(2)}) async-start(), calls=%async_computation.3 | async-start | bytes 2949120 | tf_op jit(solution)/shard_map/all_gather | solution.py:40
  10.4 20.2 %all-to-all-start = ((s32[128,1,2]{2,1,0:T(1,128)}), s32[128,1,2]{2,1,0:T(1,128)S(1)}, u32[]{:S(2)}, u32[]{:S(2)}) async-start(s32[128,1,2]{2,1,0:T(1,128)} %bitcast.13), calls=%async_computation | async-start | bytes 131072 | tf_op jit(solution)/shard_map/all_to_all | solution.py:121
  21.6 145.4 %all-gather.3.cloned.1.call-start = ((), (), s32[]{:S(2)}) async-start(), calls=%async_computation.2 | async-start | bytes 2949120 | tf_op jit(solution)/shard_map/all_gather | solution.py:48
  22.4 336.3 %all-reduce.6.cloned.1.call-start = ((), (), s32[]{:S(2)}) async-start(), calls=%async_computation.4 | async-start | bytes 524288 | tf_op jit(solution)/shard_map/psum | solution.py:74
  40.3 15.0 %copy-start.1 = (f32[1,2,1152,1152]{3,2,1,0:T(8,128)S(1)}, f32[1,2,1152,1152]{3,2,1,0:T(8,128)}, u32[]{:S(2)}) copy-start(f32[1,2,1152,1152]{3,2,1,0:T(8,128)} %param.8) | copy-start | bytes 31850500
  47.6 7.7 %copy-start.4 = (f32[1,2,256,1152]{3,2,1,0:T(8,128)S(1)}, f32[1,2,256,1152]{3,2,1,0:T(8,128)}, u32[]{:S(2)}) copy-start(f32[1,2,256,1152]{3,2,1,0:T(8,128)} %all-gather.5.cloned.1.call-done) | copy-start | bytes 7077892
  159.1 48.3 %collective-permute-start = (f32[40,256]{1,0:T(8,128)}, f32[40,256]{1,0:T(8,128)}, u32[]{:S(2)}, u32[]{:S(2)}) collective-permute-start(f32[40,256]{1,0:T(8,128)} %fusion), channel_id=1, source_target_pairs={{0,1},{1,2},{2,3},{3,16},{16,17},{17,18},{18,19},{19,32},{32,33},{... | collective-permute-start | bytes 122888
  161.0 46.4 %collective-permute-start.1 = (f32[40,256]{1,0:T(8,128)}, f32[40,256]{1,0:T(8,128)}, u32[]{:S(2)}, u32[]{:S(2)}) collective-permute-start(f32[40,256]{1,0:T(8,128)} %fusion), channel_id=1, source_target_pairs={{0,2},{1,3},{2,16},{3,17},{16,18},{17,19},{18,32},{19,33},{32,34},... | collective-permute-start | bytes 122888
  162.9 44.5 %collective-permute-start.2 = (f32[40,256]{1,0:T(8,128)}, f32[40,256]{1,0:T(8,128)}, u32[]{:S(2)}, u32[]{:S(2)}) collective-permute-start(f32[40,256]{1,0:T(8,128)} %fusion), channel_id=1, source_target_pairs={{0,3},{1,16},{2,17},{3,18},{16,19},{17,32},{18,33},{19,34},{32,35}... | collective-permute-start | bytes 122888
  165.5 41.9 %collective-permute-start.3 = (f32[4,256]{1,0:T(4,128)S(1)}, f32[4,256]{1,0:T(4,128)S(1)}, u32[]{:S(2)}, u32[]{:S(2)}) collective-permute-start(f32[4,256]{1,0:T(4,128)S(1)} %slice.66), channel_id=1, source_target_pairs={{0,16},{1,17},{2,18},{3,19},{16,32},{17,33},{18,34},{19,35},{32,48... | collective-permute-start | bytes 12296
  167.0 2.7 copy-start.2
  169.7 20.4 %slice-start = ((s8[10616832]{0:T(1024)(128)(4,1)}), s8[4194304]{0:T(1024)(128)(4,1)S(1)}, s32[]{:S(2)}) async-start(s8[10616832]{0:T(1024)(128)(4,1)} %bitcast.85), calls=%async_computation.6 | async-start | bytes 8388608
  177.8 8.1 %copy-start.3 = (f32[1152,256]{1,0:T(8,128)S(1)}, f32[1152,256]{1,0:T(8,128)}, u32[]{:S(2)}) copy-start(f32[1152,256]{1,0:T(8,128)} %get-tuple-element.7) | copy-start | bytes 3538948
  177.8 12.3 %slice-start.1 = ((s8[10616832]{0:T(1024)(128)(4,1)}), s8[4194304]{0:T(1024)(128)(4,1)S(1)}, s32[]{:S(2)}) async-start(s8[10616832]{0:T(1024)(128)(4,1)} %bitcast.85), calls=%async_computation.7 | async-start | bytes 8388608
  186.0 4.2 slice-start.2
  201.5 2.7 copy-start.11
  201.7 1.1 copy-start.5
  201.8 2.4 copy-start.6
  201.8 5.7 %copy-start.10 = (f32[40,256]{1,0:T(8,128)S(1)}, f32[40,256]{1,0:T(8,128)}, u32[]{:S(2)}) copy-start(f32[40,256]{1,0:T(8,128)} %fusion) | copy-start | bytes 122884
  201.8 8.4 %copy-start.9 = (f32[256,18]{1,0:T(8,128)S(1)}, f32[256,18]{1,0:T(8,128)}, u32[]{:S(2)}) copy-start(f32[256,18]{1,0:T(8,128)} %copy.36) | copy-start | bytes 55300
  206.7 0.7 copy-start.7
  211.9 148.1 %all-to-all-start.1 = ((f32[128,2,512]{2,1,0:T(2,128)}), f32[128,2,512]{2,1,0:T(2,128)S(1)}, u32[]{:S(2)}, u32[]{:S(2)}) async-start(f32[128,2,512]{2,1,0:T(2,128)} %copy.38), calls=%async_computation.1 | async-start | bytes 1048576 | tf_op jit(solution)/shard_map/all_to_all | solution.py:114
  225.2 239.3 %all-reduce.8.cloned.1.call-start = ((), (), s32[]{:S(2)}) async-start(), calls=%async_computation.5 | async-start | bytes 2359296
  229.4 129.3 %copy-start.8 = (f32[256,128]{1,0:T(8,128)S(1)}, f32[256,128]{1,0:T(8,128)}, u32[]{:S(2)}) copy-start(f32[256,128]{1,0:T(8,128)} %param.15) | copy-start | bytes 393220
Sparse Core Ops, SparseCore 0:
  9.7 30.5 all-gather.4
  41.9 32.4 all-gather.2
  207.5 151.1 all-reduce.5
  361.8 102.6 all-reduce.7
where the time goes:
time: 480 us; the launch traced here: 473 us
  waiting for transfers between devices  244 us (51%)
  blocking collectives  91.4 us (19%)
  matrix products  65.2 us (14%)
  starting transfers between devices  31.7 us (7%)
  between operations  16.2 us (3%)
  local copies, waits for them, and re-layouts  15.9 us (3%)
  other arithmetic  8.45 us (2%)
    psum x1, waiting for transfers between devices, body(): pivot_density = lax.psum(pivot_term, ('pole', 'row', 'col'))  128 us
    unnamed x9, waiting for transfers between devices  103 us
    unnamed x1, blocking collectives  91.4 us
    dot_general x10, matrix products, matmul(): jnp.dot(left, right, precision=lax.Precision.HIGHEST, preferred_element_t...  37.2 us
    dot_general x4, matrix products, contract_last(): lax.dot_general(left, right, (((1,), (1,)), ((), ())), precision=lax.Prec...  27.4 us
    all_to_all x1, starting transfers between devices, body(): lax.all_to_all(send_values.reshape(devices_all, capacity, block_rows * su...  13.3 us
    all_to_all x1, starting transfers between devices, body(): lax.all_to_all(send_ids.reshape(devices_all, capacity), ('pole', 'row', '...  11.2 us
  transfers between devices with their start and end apart: 10, of which 4 were waited for; matrix products, arithmetic and copies ran while one was open for 37% of the time, Pallas kernels for 0%

commit v1 on v0

v1 whole, which is shorter than its diff:
```python
import jax
import jax.numpy as jnp
from jax import lax
from jax.experimental import pallas as pl
from jax.experimental.pallas import tpu as pltpu
from jax.sharding import PartitionSpec as P

MESH = pl.DeviceIdType.MESH
F32 = jnp.float32
BF16 = jnp.bfloat16
T = 1152
S = 256
Q = 64
NB = 18
TOPK = 6
DEV = 128
CHUNKS = ((0, 512), (512, 512), (1024, 128))
BLK = 288
SUB = 72
W = T + S


def nt(a, b):
    return lax.dot_general(a, b, (((1,), (1,)), ((), ())), preferred_element_type=F32)


def nn(a, b):
    return jnp.dot(a, b, preferred_element_type=F32)


def split(v):
    hi = v.astype(BF16)
    return hi, (v - hi.astype(F32)).astype(BF16)


def rows_of(start, size):
    return pl.ds(pl.multiple_of(start, 8), size)


def kernel(
    w_ref, a_hbm, l_hbm, u_hbm, piv_ref,
    upper_out, lower_out, pv_out,
    a32, ah, al, lf, uf, relay, bl, br, uph, upl, xr, xi, xih, xil, xrh, xrl, y, lt,
    rz1, rz2, ry1, ry2, rx, cb, rc, ru1, ru2, rv1, rv2, pb,
    sends, recvs, locs,
):
    pole, row, col = lax.axis_index("pole"), lax.axis_index("row"), lax.axis_index("col")
    x_lo, z = pole // 4, pole % 4
    x_hi, core = row // 2, row % 2
    x = x_hi * 2 + x_lo

    def at_x(v):
        return ((v % 2) * 4 + z, (v // 2) * 2 + core, col)

    def row_x(v):
        return (v // 2) * 2 + core

    xp, xm, x2 = (x + 1) % 4, (x + 3) % 4, (x + 2) % 4
    yp, ym, y2 = (col + 1) % 4, (col + 3) % 4, (col + 2) % 4
    zp, zm, z2 = (z + 1) % 4, (z + 3) % 4, (z + 2) % 4
    d_core = (pole, x_hi * 2 + 1 - core, col)
    d_xp, d_xm = at_x(xp), at_x(xm)
    d_yp, d_ym, d_y2 = (pole, row, yp), (pole, row, ym), (pole, row, y2)
    d_zp, d_zm = (x_lo * 4 + zp, row, col), (x_lo * 4 + zm, row, col)
    d_xn = at_x(x_hi * 2 + 1 - x_lo)
    started = []

    def send(src, dst, dev):
        n = len(started)
        c = pltpu.make_async_remote_copy(
            src_ref=src, dst_ref=dst, send_sem=sends.at[n], recv_sem=recvs.at[n],
            device_id=dev, device_id_type=MESH,
        )
        c.start()
        started.append(c)
        return c

    local_a = []
    for b in range(4):
        rs = slice(b * BLK, (b + 1) * BLK)
        c = pltpu.make_async_copy(a_hbm.at[0, :, rs, :], a32.at[:, rs, :], locs.at[b])
        local_a.append(c)
    local_l = pltpu.make_async_copy(l_hbm.at[0], lf.at[row], locs.at[4])
    local_u = pltpu.make_async_copy(u_hbm.at[0], uf.at[col], locs.at[5])
    local_l.start()
    local_a[0].start()
    local_a[1].start()

    barrier = pltpu.get_barrier_semaphore()
    for dev in (d_core, d_xp, d_xm, d_yp, d_ym, d_y2, d_zp, d_zm):
        pl.semaphore_signal(barrier, inc=1, device_id=dev, device_id_type=MESH)
    pl.semaphore_wait(barrier, 8)

    def lanes(k):
        return pl.ds(CHUNKS[k][0], CHUNKS[k][1])

    def l_own(k):
        return (
            send(l_hbm.at[0, 0, :, lanes(k)], relay.at[0, :, lanes(k)], d_xp),
            send(l_hbm.at[0, 1, :, lanes(k)], relay.at[1, :, lanes(k)], d_xm),
        )

    def l_relay(k, own):
        own[0].wait_recv()
        p = send(relay.at[0, :, lanes(k)], lf.at[row_x(xm), 0, :, lanes(k)], d_xp)
        own[1].wait_recv()
        m = send(relay.at[1, :, lanes(k)], lf.at[row_x(xp), 1, :, lanes(k)], d_xm)
        return p, m

    far = (1 - x_hi) * 2 + core

    def l_share(k, pair):
        pair[0].wait_recv()
        pair[1].wait_recv()
        return send(lf.at[far, :, :, lanes(k)], lf.at[far, :, :, lanes(k)], d_core)

    def u_own(k):
        return (
            send(u_hbm.at[0, :, :, lanes(k)], uf.at[col, :, :, lanes(k)], d_yp),
            send(u_hbm.at[0, :, :, lanes(k)], uf.at[col, :, :, lanes(k)], d_ym),
        )

    def u_forward(k, own):
        own[0].wait_recv()
        p = send(uf.at[ym, 0, :, lanes(k)], uf.at[ym, 0, :, lanes(k)], d_yp)
        own[1].wait_recv()
        m = send(uf.at[yp, 1, :, lanes(k)], uf.at[yp, 1, :, lanes(k)], d_ym)
        return p, m

    l_near = send(l_hbm.at[0], lf.at[row], d_core)
    lo = [l_own(0)]
    uo = [u_own(0)]
    lo.append(l_own(1))
    uo.append(u_own(1))
    local_a[2].start()
    local_a[3].start()
    local_u.start()

    w_re, w_im = w_ref[0, 0], w_ref[0, 1]

    def build(dst, slot, q, lane):
        re, im = lf[slot, 0, :, lane], lf[slot, 1, :, lane]
        a, b = pl.ds(q * Q, Q), pl.ds(2 * Q + q * Q, Q)
        rh, rl = split(re)
        ih, il = split(im)
        dst[0, a, lane], dst[1, a, lane] = rh, rl
        dst[0, b, lane], dst[1, b, lane] = ih, il
        dst[2, a, lane], dst[3, a, lane] = -ih, -il
        dst[2, b, lane], dst[3, b, lane] = rh, rl

    def product(rs, lane, b):
        acc = nt(ah[0, rs, lane], b[0, :, lane])
        acc = acc + nt(ah[0, rs, lane], b[1, :, lane])
        acc = acc + nt(al[0, rs, lane], b[0, :, lane])
        acc = acc + nt(ah[1, rs, lane], b[2, :, lane])
        acc = acc + nt(ah[1, rs, lane], b[3, :, lane])
        acc = acc + nt(al[1, rs, lane], b[2, :, lane])
        return acc

    def split_a(b):
        local_a[b].wait()

        @pl.loop(0, BLK // 16)
        def _(i):
            rs = pl.ds(pl.multiple_of(b * BLK + i * 16, 16), 16)
            for part in range(2):
                hi, low = split(a32[part, rs, :])
                ah[part, rs, :] = hi
                al[part, rs, :] = low

    whole = pl.ds(0, T)

    def near(b):
        rs = pl.ds(b * BLK, BLK)
        acc = product(rs, whole, bl)
        xr[x_hi, rs, :] = acc[:, :128]
        xi[x_hi, rs, :] = acc[:, 128:]

    local_l.wait()
    l_near.wait_recv()
    for q in range(2):
        build(bl, x_hi * 2 + q, q, whole)
    split_a(0)
    near(0)
    split_a(1)
    lr = [l_relay(0, lo[0])]
    lo.append(l_own(2))
    near(1)
    split_a(2)
    lr.append(l_relay(1, lo[1]))
    uf_moves = [u_forward(0, uo[0])]
    uo.append(u_own(2))
    near(2)
    ls = [l_share(0, lr[0])]
    lr.append(l_relay(2, lo[2]))
    split_a(3)
    near(3)

    def far_chunk(k):
        for q in range(2):
            build(br, (1 - x_hi) * 2 + q, q, lanes(k))

        @pl.loop(0, 4)
        def _(b):
            rs = pl.ds(pl.multiple_of(b * BLK, 16), BLK)
            acc = product(rs, lanes(k), br)
            if k == 0:
                xr[1 - x_hi, rs, :] = acc[:, :128]
                xi[1 - x_hi, rs, :] = acc[:, 128:]
            else:
                xr[1 - x_hi, rs, :] += acc[:, :128]
                xi[1 - x_hi, rs, :] += acc[:, 128:]

    ls[0].wait_recv()
    far_chunk(0)
    ls.append(l_share(1, lr[1]))
    uf_moves.append(u_forward(1, uo[1]))
    ls.append(l_share(2, lr[2]))
    ls[1].wait_recv()
    far_chunk(1)
    uf_moves.append(u_forward(2, uo[2]))
    ls[2].wait_recv()
    far_chunk(2)

    @pl.loop(0, 4)
    def _(b):
        rs = pl.ds(pl.multiple_of(b * BLK, 16), BLK)
        for h in range(2):
            lt[h, rs, :] = -(w_re * xi[h, rs, :] + w_im * xr[h, rs, :])

    def zblk(b):
        return rows_of(b * BLK, BLK)

    c1p = send(lt.at[0, zblk(z2), :], rz1.at[0], d_zp)
    c1m = send(lt.at[1, zblk(z2), :], rz1.at[1], d_zm)

    local_u.wait()

    def upper_chunk(k):
        lane = lanes(k)
        for q in range(4):
            re, im = uf[q, 0, :, lane], uf[q, 1, :, lane]
            rs = pl.ds(q * Q, Q)
            for part, v in ((0, w_re * re - w_im * im), (1, w_re * im + w_im * re)):
                hi, low = split(v)
                uph[part, rs, lane] = hi
                upl[part, rs, lane] = low
        acc = nn(uph[0, :, lane], ah[1, lane, :])
        acc = acc + nn(uph[0, :, lane], al[1, lane, :])
        acc = acc + nn(upl[0, :, lane], ah[1, lane, :])
        acc = acc + nn(uph[1, :, lane], ah[0, lane, :])
        acc = acc + nn(uph[1, :, lane], al[0, lane, :])
        acc = acc + nn(upl[1, :, lane], ah[0, lane, :])
        if k == 0:
            y[...] = acc
        else:
            y[...] += acc

    for h in range(2):
        hs = pl.ds(h * 128, 128)
        hi, low = split(xi[h])
        xih[:, hs], xil[:, hs] = hi, low
        hi, low = split(xr[h])
        xrh[:, hs], xrl[:, hs] = hi, low

    for c in uf_moves[0]:
        c.wait_recv()
    c1p.wait_recv()
    lt[0, zblk(zp), :] += rz1[0]
    c2p = send(lt.at[:, zblk(zp), :], rz2.at[0], d_zp)
    c1m.wait_recv()
    lt[1, zblk(zm), :] += rz1[1]
    c2m = send(lt.at[:, zblk(zm), :], rz2.at[1], d_zm)
    upper_chunk(0)
    for c in uf_moves[1]:
        c.wait_recv()
    upper_chunk(1)
    for c in uf_moves[2]:
        c.wait_recv()
    upper_chunk(2)

    def yblk(b):
        return rows_of(z * BLK + b * SUB, SUB)

    c2p.wait_recv()
    c2m.wait_recv()
    for h in range(2):
        lt[h, zblk(z), :] += rz2[0, h] + rz2[1, h]
    e1p = send(lt.at[0, yblk(y2), :], ry1.at[0], d_yp)
    e1m = send(lt.at[1, yblk(y2), :], ry1.at[1], d_ym)

    pv = nn(uph[0], xih[...])
    pv = pv + nn(uph[0], xil[...])
    pv = pv + nn(upl[0], xih[...])
    pv = pv + nn(uph[1], xrh[...])
    pv = pv + nn(uph[1], xrl[...])
    pv = pv + nn(upl[1], xrh[...])
    place = (
        lax.broadcasted_iota(jnp.int32, (Q, S), 1)
        == lax.broadcasted_iota(jnp.int32, (Q, S), 0) + col * Q
    ).astype(F32)
    piece = w_re * piv_ref[0, 1] + w_im * piv_ref[0, 0]
    placed = jnp.dot(piece, place, precision=lax.Precision.HIGHEST, preferred_element_type=F32)
    y_pv = y
    for g in range(32):
        rs = slice(g * 8, g * 8 + 8)
        at = (g % 2, (g // 4) % 4, ((g // 2) % 2) * 2 + g // 16)
        mine = (row == g // 8).astype(F32)
        cb[at[0], at[1], at[2], :, :T] = -y_pv[rs, :]
        cb[at[0], at[1], at[2], :, T:] = pv[rs, :] + mine * placed[(g % 8) * 8 : (g % 8) * 8 + 8, :]
    to_core = send(cb.at[1 - core], rc, d_core)

    e1p.wait_recv()
    lt[0, yblk(yp), :] += ry1[0]
    e2p = send(lt.at[:, yblk(yp), :], ry2.at[0], d_yp)
    e1m.wait_recv()
    lt[1, yblk(ym), :] += ry1[1]
    e2m = send(lt.at[:, yblk(ym), :], ry2.at[1], d_ym)

    to_core.wait_recv()

    @pl.loop(0, 4)
    def _(b):
        cb[core, b] += rc[b]

    f1p = send(cb.at[core, z2, pl.ds(0, 2)], ru1.at[0], d_zp)
    f1m = send(cb.at[core, z2, pl.ds(2, 2)], ru1.at[1], d_zm)

    e2p.wait_recv()
    e2m.wait_recv()
    for h in range(2):
        lt[h, yblk(col), :] += ry2[0, h] + ry2[1, h]
    g1 = send(lt.at[:, yblk(col), :], rx, d_xn)

    f1p.wait_recv()
    cb[core, zp, 0:2] += ru1[0]
    f2p = send(cb.at[core, zp], ru2.at[0], d_zp)
    f1m.wait_recv()
    cb[core, zm, 2:4] += ru1[1]
    f2m = send(cb.at[core, zm], ru2.at[1], d_zm)

    g1.wait_recv()
    for h in range(2):
        lower_out[:, h * 128 : (h + 1) * 128] = lt[h, yblk(col), :] + rx[h]

    f2p.wait_recv()
    f2m.wait_recv()
    cb[core, z] += ru2[0] + ru2[1]
    h1p = send(cb.at[core, z, x2, :, pl.ds(0, 768)], rv1.at[0, :, pl.ds(0, 768)], d_xp)
    h1m = send(cb.at[core, z, x2, :, pl.ds(768, 640)], rv1.at[1, :, pl.ds(0, 640)], d_xm)
    h1p.wait_recv()
    cb[core, z, xp, :, :768] += rv1[0]
    h2p = send(cb.at[core, z, xp], rv2.at[0], d_xp)
    h1m.wait_recv()
    cb[core, z, xm, :, 768:] += rv1[1, :, :640]
    h2m = send(cb.at[core, z, xm], rv2.at[1], d_xm)
    h2p.wait_recv()
    h2m.wait_recv()
    total = cb[core, z, x] + rv2[0] + rv2[1]
    upper_out[...] = total[:, :T]
    pb[col] = total[:, T:]
    last = [send(pb.at[col], pb.at[col], dev) for dev in (d_yp, d_ym, d_y2)]
    for c in last:
        c.wait_recv()
    pv_out[...] = pb[0] + pb[1] + pb[2] + pb[3]
    for c in started:
        c.wait_send()


N_COPIES = 1 + 6 + 6 + 6 + 6 + 3 + 4 + 4 + 1 + 1 + 4 + 4 + 3


def dense_part(weights, tile, lower, upper, pivot):
    vmem = pl.BlockSpec(memory_space=pltpu.VMEM)
    hbm = pl.BlockSpec(memory_space=pl.ANY)
    return pl.pallas_call(
        kernel,
        out_shape=(
            jax.ShapeDtypeStruct((8, T), F32),
            jax.ShapeDtypeStruct((SUB, S), F32),
            jax.ShapeDtypeStruct((8, S), F32),
        ),
        in_specs=[pl.BlockSpec(memory_space=pltpu.SMEM), hbm, hbm, hbm, vmem],
        out_specs=(vmem, vmem, vmem),
        scratch_shapes=[
            pltpu.VMEM((2, T, T), F32),
            pltpu.VMEM((2, T, T), BF16),
            pltpu.VMEM((2, T, T), BF16),
            pltpu.VMEM((4, 2, Q, T), F32),
            pltpu.VMEM((4, 2, Q, T), F32),
            pltpu.VMEM((2, Q, T), F32),
            pltpu.VMEM((4, S, T), BF16),
            pltpu.VMEM((4, S, T), BF16),
            pltpu.VMEM((2, S, T), BF16),
            pltpu.VMEM((2, S, T), BF16),
            pltpu.VMEM((2, T, 128), F32),
            pltpu.VMEM((2, T, 128), F32),
            pltpu.VMEM((T, S), BF16),
            pltpu.VMEM((T, S), BF16),
            pltpu.VMEM((T, S), BF16),
            pltpu.VMEM((T, S), BF16),
            pltpu.VMEM((S, T), F32),
            pltpu.VMEM((2, T, 128), F32),
            pltpu.VMEM((2, BLK, 128), F32),
            pltpu.VMEM((2, 2, BLK, 128), F32),
            pltpu.VMEM((2, SUB, 128), F32),
            pltpu.VMEM((2, 2, SUB, 128), F32),
            pltpu.VMEM((2, SUB, 128), F32),
            pltpu.VMEM((2, 4, 4, 8, W), F32),
            pltpu.VMEM((4, 4, 8, W), F32),
            pltpu.VMEM((2, 2, 8, W), F32),
            pltpu.VMEM((2, 4, 8, W), F32),
            pltpu.VMEM((2, 8, 768), F32),
            pltpu.VMEM((2, 8, W), F32),
            pltpu.VMEM((4, 8, S), F32),
            pltpu.SemaphoreType.DMA((N_COPIES,)),
            pltpu.SemaphoreType.DMA((N_COPIES,)),
            pltpu.SemaphoreType.DMA((6,)),
        ],
        compiler_params=pltpu.CompilerParams(
            collective_id=0, has_side_effects=True, vmem_limit_bytes=60 << 20
        ),
    )(weights, tile, lower, upper, pivot)


def body(
    inverse_tile, lower_factor, upper_factor, pivot_inverse, pole_weights, block_owners,
    basis_ancestor, basis_super,
):
    pole, row, col = lax.axis_index("pole"), lax.axis_index("row"), lax.axis_index("col")
    me = (pole * 4 + row) * 4 + col
    group = row * 32 + (pole % 4) * 8 + col * 2 + pole // 4

    owners = block_owners.T
    here = lax.dynamic_slice_in_dim(owners, group * NB, NB, 1)
    everyone = jnp.arange(DEV, dtype=jnp.int32)
    named = jnp.max((here[:, :, None] == everyone[None, None, :]).astype(F32), 0)
    before = (jnp.arange(NB)[:, None] > jnp.arange(NB)[None, :]).astype(F32)
    rank = jnp.dot(before, named)
    chosen = jnp.stack([named * (rank == slot) for slot in range(2)], 2).reshape(NB, 2 * DEV)

    mine = jnp.max((owners == me).astype(F32), 0).reshape(DEV, NB)
    place = jnp.dot(mine, before.T)
    ids = jnp.arange(DEV * NB, dtype=jnp.int32).reshape(DEV, NB)
    picked = jnp.stack(
        [jnp.sum(jnp.where((mine > 0) & (place == slot), ids, 0), 1) for slot in range(2)], 1
    )
    picked = picked.reshape(4, 4, 4, 2, 2).transpose(3, 1, 0, 2, 4).reshape(-1)
    row_ids = (picked[:, None] * 2 + jnp.arange(2, dtype=jnp.int32)[None, :]).reshape(-1)
    ancestor_rows = jnp.take(basis_ancestor, row_ids, axis=0, mode="clip")

    upper_density, lower_rows, pivot_rows = dense_part(
        pole_weights, inverse_tile, lower_factor, upper_factor, pivot_inverse
    )
    values = lax.dynamic_slice_in_dim(lower_rows, (pole // 4) * 36, 36, 0).reshape(NB, 2 * S)
    packed = lax.dot_general(
        chosen, values, (((0,), (0,)), ((), ())),
        precision=lax.Precision.HIGHEST, preferred_element_type=F32,
    ).reshape(DEV, 2, 2 * S)
    pivot_part = lax.dynamic_slice_in_dim(pivot_rows, col * 2, 2, 0).reshape(1, 1, 2 * S)
    packed = jnp.concatenate([packed, jnp.broadcast_to(pivot_part, (DEV, 1, 2 * S))], 1)
    got = lax.all_to_all(packed, ("pole", "row", "col"), split_axis=0, concat_axis=0, tiled=True)
    received = got[:, :2].reshape(-1, S)
    pivot_density = got[:, 2].reshape(S, S)
    high = lax.Precision.HIGH
    projected = jnp.dot(received, basis_super, precision=high, preferred_element_type=F32)
    charge = jnp.sum(ancestor_rows * projected, 0) + jnp.sum(
        basis_super
        * jnp.dot(pivot_density, basis_super, precision=high, preferred_element_type=F32),
        0,
    )
    return (upper_density, charge)


def solution(mesh):
    placed = (
        P("pole", None, "row", "col"),
        P("pole", None, "row", "col"),
        P("pole", None, "col", "row"),
        P("pole", None, "row", "col"),
        P("pole", None),
        P(),
        P(None, ("pole", "row", "col")),
        P(None, ("pole", "row", "col")),
    )
    return jax.shard_map(
        body,
        mesh=mesh,
        in_specs=placed,
        out_specs=(P(("pole", "row"), "col"), P(("pole", "row", "col"))),
        check_vma=False,
    )
```

time: 480 us -> 113 us (0.24); the launches traced: 473 us -> 112 us
  waiting for transfers between devices: 244 us -> 14.1 us
  blocking collectives: 91.4 us -> 0 us
  Pallas kernels: 0 us -> 71 us
  matrix products: 65.2 us -> 2.65 us
  starting transfers between devices: 31.7 us -> 7.87 us
  between operations: 16.2 us -> 0.84 us
  other arithmetic: 8.45 us -> 0.84 us
    psum x1 -> x0, waiting for transfers between devices: 128 us -> none  [body(): pivot_density = lax.psum(pivot_term, ('pole', 'row', 'col'))]
    unnamed x9 -> x0, waiting for transfers between devices: 103 us -> none
    unnamed x1 -> x0, blocking collectives: 91.4 us -> none
    pallas_call x0 -> x1, Pallas kernels: none -> 71 us  [dense_part(): pl.pallas_call(kernel, out_shape=(jax.ShapeDtypeStruct((8, T), F32), jax....]
    dot_general x15 -> x5, matrix products: 65.2 us -> 2.65 us  [the longest x1 1.5 us: body(): jnp.dot(received, basis_super, precision=high, preferred_element_type=F32)]
    all_to_all x2 -> x1, starting transfers between devices: 24.4 us -> 7.87 us  [body(): lax.all_to_all(packed, ('pole', 'row', 'col'), split_axis=0, concat_axis=...]
    all_to_all x2 -> x1, waiting for transfers between devices: 4.14 us -> 14.1 us  [body(): lax.all_to_all(packed, ('pole', 'row', 'col'), split_axis=0, concat_axis=...]
    all_gather x2 -> x0, waiting for transfers between devices: 8.92 us -> none  [the longest x1 8.89 us: body(): fragment = lax.all_gather(lower_factor, 'row', axis=2, tiled=True)]
  transfers between devices with their start and end apart: 10 -> 1, of which waited for: 4 -> 1; matrix products, arithmetic and copies ran while one was open for 37% -> 3% of each run, Pallas kernels for 0% -> 0%
where the time goes in v1:
time: 113 us; the launch traced here: 112 us
  Pallas kernels  71 us (63%)
  local copies, waits for them, and re-layouts  14.2 us (13%)
  waiting for transfers between devices  14.1 us (12%)
  starting transfers between devices  7.87 us (7%)
  matrix products  2.65 us (2%)
    pallas_call x1, Pallas kernels, dense_part(): pl.pallas_call(kernel, out_shape=(jax.ShapeDtypeStruct((8, T), F32), jax....  71 us
    all_to_all x1, waiting for transfers between devices, body(): lax.all_to_all(packed, ('pole', 'row', 'col'), split_axis=0, concat_axis=...  14.1 us
    all_to_all x1, starting transfers between devices, body(): lax.all_to_all(packed, ('pole', 'row', 'col'), split_axis=0, concat_axis=...  7.87 us
  transfers between devices with their start and end apart: 1, of which 1 were waited for; matrix products, arithmetic and copies ran while one was open for 3% of the time, Pallas kernels for 0%

profile of v1, /device:TPU:0, one launch (start us, length us, event | category | flops | bytes accessed | tf_op | source)
XLA Modules:
  0.0 111.6 jit_solution(16404025417159672374)
XLA Ops:
  0.6 0.0 copy-start
  0.7 0.9 dynamic-slice_bitcast_fusion
  1.6 0.1 convert_reduce_fusion
  1.7 0.1 select_bitcast_fusion.1
  1.8 0.1 copy.22
  2.0 71.0 %shard_map.95 = (f32[8,1152]{1,0:T(8,128)}, f32[72,256]{1,0:T(8,128)}, f32[8,256]{1,0:T(8,128)}) custom-call(f32[1,2]{1,0:T(1,128)} %w_ref.1, f32[1,2,1152,1152]{3,2,1,0:T(8,128)} %a_hbm.1, f32[1,2,64,1152]{3,2,1,0:T(8,128)} %l_hbm.1, f32[1,2,64,1152]{3,2,1,0:T(8,128)} %u_hbm.1, f32[1,2,64,64]{3,2,1,0:T(8,128)} %piv_ref.1), custom_call_target="tpu_custom_call" | custom-call | tf_op jit(solution)/shard_map/pallas_call | solution.py:376
  73.0 0.8 constant_dynamic-slice_fusion
  73.9 0.7 dynamic-slice_bitcast_fusion.1
  74.6 0.6 fusion.2
  75.2 0.1 pad_maximum_fusion
  75.2 0.0 copy-start.2
  75.2 1.5 %copy.24 = f32[128,3,512]{2,1,0:T(4,128)} copy(f32[128,3,512]{2,0,1:T(8,128)S(1)} %pad_maximum_fusion) | data formatting | bytes 1572864 | tf_op jit(solution)/shard_map/concatenate | solution.py:461
  76.8 7.9 %all-to-all-start = ((f32[128,3,512]{2,1,0:T(4,128)}), f32[128,3,512]{2,1,0:T(4,128)S(1)}, u32[]{:S(2)}, u32[]{:S(2)}) async-start(f32[128,3,512]{2,1,0:T(4,128)} %copy.24), calls=%async_computation | async-start | bytes 2097152 | tf_op jit(solution)/shard_map/all_to_all | solution.py:462
  84.7 0.1 reshape.72
  84.8 0.1 copy.20
  84.9 0.2 select_reduce_fusion.1
  85.1 0.2 stack.18
  85.3 0.2 stack.19
  85.5 0.5 copy.21
  86.0 0.1 mul.56
  86.1 0.1 iota_add_fusion
  86.2 0.1 reshape.81
  86.4 1.6 %gather_fusion = f32[512,128]{1,0:T(8,128)} fusion(f32[4608,128]{1,0:T(8,128)S(1)} %copy-done, s32[1024]{0:T(1024)S(1)} %pad_clamp_fusion), kind=kCustom, calls=%fused_computation | custom fusion | bytes 526336 | tf_op jit(solution)/shard_map/jit(_take)/gather | solution.py:450
  88.1 14.1 %all-to-all-done = f32[128,3,512]{2,1,0:T(4,128)S(1)} async-done(((f32[128,3,512]{2,1,0:T(4,128)}), f32[128,3,512]{2,1,0:T(4,128)S(1)}, u32[]{:S(2)}, u32[]{:S(2)}) %all-to-all-start) | async-done | bytes 786464 | tf_op jit(solution)/shard_map/all_to_all | solution.py:462
  102.2 1.0 slice.10
  103.2 2.2 %reshape.78 = f32[512,256]{1,0:T(8,128)} reshape(f32[128,2,512]{2,1,0:T(2,128)} %slice.10) | data formatting | bytes 1048576 | tf_op jit(solution)/shard_map/reshape | solution.py:463
  105.4 1.4 %slice_reduce_fusion = f32[128,512]{1,0:T(8,128)} fusion(f32[128,3,512]{2,1,0:T(4,128)S(1)} %all-to-all-done), kind=kLoop, calls=%fused_computation.6 | loop fusion | bytes 524288 | tf_op jit(solution)/shard_map/slice | solution.py:464
  106.9 1.0 reshape_squeeze.3
  107.9 0.3 fusion.1
  108.2 1.5 %fusion = f32[128]{0:T(128)S(1)} fusion(f32[512,128]{1,0:T(8,128)} %gather_fusion, f32[512,256]{1,0:T(8,128)} %reshape.78, f32[256,128]{1,0:T(8,128)S(1)} %copy-done.1), kind=kOutput, calls=%fused_computation.3 | convolution fusion | flops 100794240 | bytes 918016 | tf_op jit(solution)/shard_map/dot_general | solution.py:466
  109.7 0.5 add.69
  110.2 1.4 %copy.29 = f32[8,1152]{1,0:T(8,128)} copy(f32[8,1152]{1,0:T(8,128)} %get-tuple-element.14) | data formatting | bytes 73728
  (11 shorter events, 0.1 us)
Async XLA Ops:
  0.6 85.8 %copy-start = (f32[4608,128]{1,0:T(8,128)S(1)}, f32[4608,128]{1,0:T(8,128)}, u32[]{:S(2)}) copy-start(f32[4608,128]{1,0:T(8,128)} %param.14) | copy-start | bytes 7077892
  75.2 9.4 %copy-start.2 = (s32[2304,6]{0,1:T(8,128)S(1)}, s32[2304,6]{0,1:T(8,128)}, u32[]{:S(2)}) copy-start(s32[2304,6]{0,1:T(8,128)} %param.13) | copy-start | bytes 165892
  76.8 25.4 %all-to-all-start = ((f32[128,3,512]{2,1,0:T(4,128)}), f32[128,3,512]{2,1,0:T(4,128)S(1)}, u32[]{:S(2)}, u32[]{:S(2)}) async-start(f32[128,3,512]{2,1,0:T(4,128)} %copy.24), calls=%async_computation | async-start | bytes 2097152 | tf_op jit(solution)/shard_map/all_to_all | solution.py:462
  86.4 21.5 %copy-start.1 = (f32[256,128]{1,0:T(8,128)S(1)}, f32[256,128]{1,0:T(8,128)}, u32[]{:S(2)}) copy-start(f32[256,128]{1,0:T(8,128)} %param.15) | copy-start | bytes 393220

commit v2 on v1

v2 whole, which is shorter than its diff:
```python
import jax
import jax.numpy as jnp
from jax import lax
from jax.experimental import pallas as pl
from jax.experimental.pallas import tpu as pltpu
from jax.sharding import PartitionSpec as P

MESH = pl.DeviceIdType.MESH
F32 = jnp.float32
BF16 = jnp.bfloat16
T = 1152
S = 256
Q = 64
NB = 18
TOPK = 6
BAT = 8
WIDE = 288
DEV = 128
CHUNKS = ((0, 512), (512, 512), (1024, 128))
BLK = 288
SUB = 72
FIRST = 40
LEFT = 640


def nt(a, b):
    return lax.dot_general(a, b, (((1,), (1,)), ((), ())), preferred_element_type=F32)


def nn(a, b):
    return jnp.dot(a, b, preferred_element_type=F32)


def split(v):
    hi = v.astype(BF16)
    return hi, (v - hi.astype(F32)).astype(BF16)


def tn(a, b):
    return lax.dot_general(a, b, (((0,), (0,)), ((), ())), preferred_element_type=F32)


def iota(shape, dim):
    return lax.broadcasted_iota(jnp.int32, shape, dim)


def rows_of(start, size):
    return pl.ds(pl.multiple_of(start, 8), size)


def kernel(
    w_ref, a_hbm, l_hbm, u_hbm, piv_ref, own_ref, bs_ref, ba_hbm,
    upper_out, charge_out,
    a32, ah, al, lf, uf, relay, bl, br, uph, upl, xr, xi, xih, xil, xrh, xrl, y, lt,
    rz1, rz2, ry1, ry2, rx, ld, cb, rc, ru1, ru2, rv1, rv2,
    pvb, pc, pz, px, pb, pfull, bsp, ba, ba8, sel, pk, got,
    sends, recvs, locs, asend, arecv,
):
    pole, row, col = lax.axis_index("pole"), lax.axis_index("row"), lax.axis_index("col")
    x_lo, z = pole // 4, pole % 4
    x_hi, core = row // 2, row % 2
    x = x_hi * 2 + x_lo
    me = (pole * 4 + row) * 4 + col
    group = row * 32 + z * 8 + col * 2 + x_lo

    def at_x(v):
        return ((v % 2) * 4 + z, (v // 2) * 2 + core, col)

    def at_y(v):
        return (pole, row, v)

    def at_z(v):
        return (x_lo * 4 + v, row, col)

    def row_x(v):
        return (v // 2) * 2 + core

    xp, xm, x2 = (x + 1) % 4, (x + 3) % 4, (x + 2) % 4
    yp, ym, y2 = (col + 1) % 4, (col + 3) % 4, (col + 2) % 4
    zp, zm, z2 = (z + 1) % 4, (z + 3) % 4, (z + 2) % 4
    d_core = (pole, x_hi * 2 + 1 - core, col)
    d_xp, d_xm = at_x(xp), at_x(xm)
    d_yp, d_ym = at_y(yp), at_y(ym)
    d_zp, d_zm = at_z(zp), at_z(zm)
    d_xn = at_x(x_hi * 2 + 1 - x_lo)
    started = []

    def send(src, dst, dev):
        n = len(started)
        c = pltpu.make_async_remote_copy(
            src_ref=src, dst_ref=dst, send_sem=sends.at[n], recv_sem=recvs.at[n],
            device_id=dev, device_id_type=MESH,
        )
        c.start()
        started.append(c)
        return c

    local_a = []
    for b in range(4):
        rs = slice(b * BLK, (b + 1) * BLK)
        c = pltpu.make_async_copy(a_hbm.at[0, :, rs, :], a32.at[:, rs, :], locs.at[b])
        local_a.append(c)
    local_l = pltpu.make_async_copy(l_hbm.at[0], lf.at[row], locs.at[4])
    local_u = pltpu.make_async_copy(u_hbm.at[0], uf.at[col], locs.at[5])
    local_ba = pltpu.make_async_copy(ba_hbm, ba, locs.at[6])
    local_l.start()
    local_a[0].start()
    local_a[1].start()

    barrier = pltpu.get_barrier_semaphore()
    greet = (d_core, d_xp, d_xm, at_x(x2), d_yp, d_ym, at_y(y2), d_zp, d_zm, at_z(z2))
    for dev in greet:
        pl.semaphore_signal(barrier, inc=1, device_id=dev, device_id_type=MESH)
    pl.semaphore_wait(barrier, len(greet))

    def lanes(k):
        return pl.ds(CHUNKS[k][0], CHUNKS[k][1])

    def l_own(k):
        return (
            send(l_hbm.at[0, 0, :, lanes(k)], relay.at[0, :, lanes(k)], d_xp),
            send(l_hbm.at[0, 1, :, lanes(k)], relay.at[1, :, lanes(k)], d_xm),
        )

    def l_relay(k, own):
        own[0].wait_recv()
        p = send(relay.at[0, :, lanes(k)], lf.at[row_x(xm), 0, :, lanes(k)], d_xp)
        own[1].wait_recv()
        m = send(relay.at[1, :, lanes(k)], lf.at[row_x(xp), 1, :, lanes(k)], d_xm)
        return p, m

    far = (1 - x_hi) * 2 + core

    def l_share(k, pair):
        pair[0].wait_recv()
        pair[1].wait_recv()
        return send(lf.at[far, :, :, lanes(k)], lf.at[far, :, :, lanes(k)], d_core)

    def u_own(k):
        return (
            send(u_hbm.at[0, :, :, lanes(k)], uf.at[col, :, :, lanes(k)], d_yp),
            send(u_hbm.at[0, :, :, lanes(k)], uf.at[col, :, :, lanes(k)], d_ym),
        )

    def u_forward(k, own):
        own[0].wait_recv()
        p = send(uf.at[ym, 0, :, lanes(k)], uf.at[ym, 0, :, lanes(k)], d_yp)
        own[1].wait_recv()
        m = send(uf.at[yp, 1, :, lanes(k)], uf.at[yp, 1, :, lanes(k)], d_ym)
        return p, m

    l_near = send(l_hbm.at[0], lf.at[row], d_core)
    lo = [l_own(0)]
    uo = [u_own(0)]
    lo.append(l_own(1))
    uo.append(u_own(1))
    local_a[2].start()
    local_a[3].start()
    local_u.start()
    local_ba.start()

    w_re, w_im = w_ref[0, 0], w_ref[0, 1]

    def build(dst, slot, q, lane):
        re, im = lf[slot, 0, :, lane], lf[slot, 1, :, lane]
        a, b = pl.ds(q * Q, Q), pl.ds(2 * Q + q * Q, Q)
        rh, rl = split(re)
        ih, il = split(im)
        dst[0, a, lane], dst[1, a, lane] = rh, rl
        dst[0, b, lane], dst[1, b, lane] = ih, il
        dst[2, a, lane], dst[3, a, lane] = -ih, -il
        dst[2, b, lane], dst[3, b, lane] = rh, rl

    def product(rs, lane, b):
        acc = nt(ah[0, rs, lane], b[0, :, lane])
        acc = acc + nt(ah[0, rs, lane], b[1, :, lane])
        acc = acc + nt(al[0, rs, lane], b[0, :, lane])
        acc = acc + nt(ah[1, rs, lane], b[2, :, lane])
        acc = acc + nt(ah[1, rs, lane], b[3, :, lane])
        acc = acc + nt(al[1, rs, lane], b[2, :, lane])
        return acc

    def split_a(b):
        local_a[b].wait()

        @pl.loop(0, BLK // 16)
        def _(i):
            rs = pl.ds(pl.multiple_of(b * BLK + i * 16, 16), 16)
            for part in range(2):
                hi, low = split(a32[part, rs, :])
                ah[part, rs, :] = hi
                al[part, rs, :] = low

    whole = pl.ds(0, T)

    def near(b):
        rs = pl.ds(b * BLK, BLK)
        acc = product(rs, whole, bl)
        xr[x_hi, rs, :] = acc[:, :128]
        xi[x_hi, rs, :] = acc[:, 128:]

    halves = (x_hi, 1 - x_hi)

    def lower_term(n):
        h = halves[n]

        @pl.loop(0, 4)
        def _(b):
            rs = pl.ds(pl.multiple_of(b * BLK, 16), BLK)
            lt[h, rs, :] = -(w_re * xi[h, rs, :] + w_im * xr[h, rs, :])

    def z_at(b):
        return b * BLK

    def y_at(b):
        return z * BLK + b * SUB

    z_ring = (z_at, BLK, 144, (zp, zm, z2, z), (d_zp, d_zm), rz1, rz2)
    y_ring = (y_at, SUB, FIRST, (yp, ym, y2, col), (d_yp, d_ym), ry1, ry2)

    def ring1(n, ring):
        at, size, first, (p, m, two, own), (dp, dm), r1, r2 = ring
        h = halves[n]
        return (
            send(lt.at[h, rows_of(at(two), first), :], r1.at[n, pl.ds(0, first), :], dp),
            send(
                lt.at[h, rows_of(at(two) + first, size - first), :],
                r1.at[n, pl.ds(first, size - first), :], dm,
            ),
        )

    def ring2(n, ring, before):
        at, size, first, (p, m, two, own), (dp, dm), r1, r2 = ring
        h = halves[n]
        before[0].wait_recv()
        lt[h, rows_of(at(p), first), :] += r1[n, 0:first]
        a = send(lt.at[h, rows_of(at(p), size), :], r2.at[n, 0], dp)
        before[1].wait_recv()
        lt[h, rows_of(at(m) + first, size - first), :] += r1[n, first:size]
        return a, send(lt.at[h, rows_of(at(m), size), :], r2.at[n, 1], dm)

    def ring3(n, ring, before):
        at, size, first, (p, m, two, own), (dp, dm), r1, r2 = ring
        before[0].wait_recv()
        before[1].wait_recv()
        lt[halves[n], rows_of(at(own), size), :] += r2[n, 0] + r2[n, 1]

    def x_swap(n):
        return send(lt.at[halves[n], rows_of(y_at(col), SUB), :], rx.at[n], d_xn)

    def x_add(n, before):
        before.wait_recv()
        ld[halves[n]] = lt[halves[n], rows_of(y_at(col), SUB), :] + rx[n]

    def upper_chunk(k):
        lane = lanes(k)
        for q in range(4):
            re, im = uf[q, 0, :, lane], uf[q, 1, :, lane]
            rs = pl.ds(q * Q, Q)
            for part, v in ((0, w_re * re - w_im * im), (1, w_re * im + w_im * re)):
                hi, low = split(v)
                uph[part, rs, lane] = hi
                upl[part, rs, lane] = low
        acc = nn(uph[0, :, lane], ah[1, lane, :])
        acc = acc + nn(uph[0, :, lane], al[1, lane, :])
        acc = acc + nn(upl[0, :, lane], ah[1, lane, :])
        acc = acc + nn(uph[1, :, lane], ah[0, lane, :])
        acc = acc + nn(uph[1, :, lane], al[0, lane, :])
        acc = acc + nn(upl[1, :, lane], ah[0, lane, :])
        if k == 0:
            y[...] = acc
        else:
            y[...] += acc

    def far_chunk(k):
        for q in range(2):
            build(br, (1 - x_hi) * 2 + q, q, lanes(k))

        @pl.loop(0, 4)
        def _(b):
            rs = pl.ds(pl.multiple_of(b * BLK, 16), BLK)
            acc = product(rs, lanes(k), br)
            if k == 0:
                xr[1 - x_hi, rs, :] = acc[:, :128]
                xi[1 - x_hi, rs, :] = acc[:, 128:]
            else:
                xr[1 - x_hi, rs, :] += acc[:, :128]
                xi[1 - x_hi, rs, :] += acc[:, 128:]

    def choose_rows():
        mine = own_ref[group // 16].astype(F32).astype(BF16)
        here = nn(
            mine,
            (iota((WIDE, NB), 0) == (group % 16) * NB + iota((WIDE, NB), 1)).astype(F32).astype(BF16),
        )
        owner = iota((2 * DEV, NB), 0)
        named = jnp.zeros((2 * DEV, NB), F32)
        for t in range(TOPK):
            hit = here[t : t + 1, :] == (owner // 2).astype(F32)
            named = jnp.maximum(named, hit.astype(F32))
        earlier = (iota((NB, NB), 0) < iota((NB, NB), 1)).astype(F32).astype(BF16)
        rank = nn(named.astype(BF16), earlier)
        chosen = named * (rank == (owner % 2).astype(F32)).astype(F32)
        spot = iota((NB, 2 * SUB), 1) % SUB
        spread = (
            (spot // 36 == x_lo) & ((spot % 36) // 2 == iota((NB, 2 * SUB), 0))
        ).astype(F32)
        wide = nn(chosen.astype(BF16), spread.astype(BF16))
        out = iota((8 * DEV, 2 * DEV), 0)
        repeat = (iota((8 * DEV, 2 * DEV), 1) == (out // 8) * 2 + (out // 2) % 2).astype(F32)
        full = nn(repeat.astype(BF16), wide.astype(BF16))
        ro, co = iota((8 * DEV, 2 * SUB), 0), iota((8 * DEV, 2 * SUB), 1)
        keep = ((ro // 4) % 2 == co // SUB) & (ro % 2 == co % 2)
        sel[...] = jnp.where(keep, full, 0.0).astype(BF16)

    def choose_ancestors():
        local_ba.wait()
        block = iota((WIDE, WIDE), 0), iota((WIDE, WIDE), 1)
        earlier = ((block[0] // NB == block[1] // NB) & (block[0] < block[1])).astype(F32)
        earlier = earlier.astype(BF16)
        slot = iota((8 * 16, WIDE), 0)
        wanted = slot - (slot // 4) % 2 * 4 - slot % 2

        @pl.loop(0, BAT)
        def _(b):
            owners = own_ref[b]
            mine = jnp.max((owners == me).astype(F32), 0, keepdims=True)
            rank = nn(jnp.broadcast_to(mine, (8, WIDE)).astype(BF16), earlier)[0:1, :]
            base = (iota((1, WIDE), 1) // NB * 8).astype(F32)
            key = jnp.where(mine > 0, base + 2 * rank, -8.0)
            hit = key == wanted.astype(F32)
            acc = jnp.zeros((8 * 16, 128), F32)
            for parity in range(2):
                one = (hit & (slot % 2 == parity)).astype(F32).astype(BF16)
                v = ba[pl.ds(b * 2 * WIDE + parity, WIDE, stride=2), :]
                hi, low = split(v)
                acc = acc + nn(one, hi) + nn(one, low)
            ba8[rows_of(b * 128, 128), :] = acc

    def exchange():
        v = ld[...].reshape(2 * SUB, 128)
        hi, low = split(v)
        rest = (v - hi.astype(F32) - low.astype(F32)).astype(BF16)
        packed = nn(sel[...], hi) + nn(sel[...], low) + nn(sel[...], rest)
        pk[...] = packed.reshape(DEV, 8, 128)
        got[group] = pk[me]

        @pl.loop(1, DEV)
        def _(d):
            t = (me + d) % DEV
            pltpu.make_async_remote_copy(
                src_ref=pk.at[t], dst_ref=got.at[group], send_sem=asend.at[0], recv_sem=arecv.at[0],
                device_id=(t // 16, (t // 4) % 4, t % 4), device_id_type=MESH,
            ).start()

    def three(a, b):
        ahi, alo = split(a)
        bhi, blo = split(b)
        return nn(ahi, bhi) + nn(ahi, blo) + nn(alo, bhi)

    local_l.wait()
    l_near.wait_recv()
    for q in range(2):
        build(bl, x_hi * 2 + q, q, whole)
    split_a(0)
    near(0)
    split_a(1)
    lr = [l_relay(0, lo[0])]
    lo.append(l_own(2))
    near(1)
    split_a(2)
    lr.append(l_relay(1, lo[1]))
    uf_moves = [u_forward(0, uo[0])]
    uo.append(u_own(2))
    near(2)
    ls = [l_share(0, lr[0])]
    lr.append(l_relay(2, lo[2]))
    split_a(3)
    near(3)
    lower_term(0)
    zn = ring1(0, z_ring)
    ls.append(l_share(1, lr[1]))
    ls[0].wait_recv()
    far_chunk(0)
    zn = ring2(0, z_ring, zn)
    uf_moves.append(u_forward(1, uo[1]))
    ls.append(l_share(2, lr[2]))
    ls[1].wait_recv()
    far_chunk(1)
    uf_moves.append(u_forward(2, uo[2]))
    ring3(0, z_ring, zn)
    yn = ring1(0, y_ring)
    ls[2].wait_recv()
    far_chunk(2)
    lower_term(1)
    zf = ring1(1, z_ring)
    local_u.wait()
    for h in range(2):
        hs = pl.ds(h * 128, 128)
        hi, low = split(xi[h])
        xih[:, hs], xil[:, hs] = hi, low
        hi, low = split(xr[h])
        xrh[:, hs], xrl[:, hs] = hi, low
    for c in uf_moves[0]:
        c.wait_recv()
    zf = ring2(1, z_ring, zf)
    yn = ring2(0, y_ring, yn)
    upper_chunk(0)
    ring3(0, y_ring, yn)
    xn = x_swap(0)
    for c in uf_moves[1]:
        c.wait_recv()
    upper_chunk(1)
    ring3(1, z_ring, zf)
    yf = ring1(1, y_ring)
    x_add(0, xn)
    for c in uf_moves[2]:
        c.wait_recv()
    upper_chunk(2)

    for g in range(32):
        at = (g % 2, (g // 4) % 4, ((g // 2) % 2) * 2 + g // 16)
        cb[at[0], at[1], at[2]] = -y[g * 8 : g * 8 + 8, :]
    to_core = send(cb.at[1 - core], rc, d_core)

    pv = nn(uph[0], xih[...])
    pv = pv + nn(uph[0], xil[...])
    pv = pv + nn(upl[0], xih[...])
    pv = pv + nn(uph[1], xrh[...])
    pv = pv + nn(uph[1], xrl[...])
    pv = pv + nn(upl[1], xrh[...])
    place = (iota((Q, S), 1) == iota((Q, S), 0) + col * Q).astype(F32)
    piece = w_re * piv_ref[0, 1] + w_im * piv_ref[0, 0]
    placed = jnp.dot(piece, place, precision=lax.Precision.HIGHEST, preferred_element_type=F32)
    for g in range(32):
        at = (g % 2, (g // 4) % 4, ((g // 2) % 2) * 2 + g // 16)
        mine = (row == g // 8).astype(F32)
        pvb[at[0], at[1], at[2]] = (
            pv[g * 8 : g * 8 + 8, :] + mine * placed[(g % 8) * 8 : (g % 8) * 8 + 8, :]
        )
    p1 = send(pvb.at[1 - core], pc, d_core)
    yf = ring2(1, y_ring, yf)

    to_core.wait_recv()

    @pl.loop(0, 4)
    def _(b):
        cb[core, b] += rc[b]

    f1p = send(cb.at[core, z2, pl.ds(0, 2)], ru1.at[0], d_zp)
    f1m = send(cb.at[core, z2, pl.ds(2, 2)], ru1.at[1], d_zm)
    p1.wait_recv()
    pvb[core] += pc[...]
    p2 = [
        send(pvb.at[core, (z + d) % 4], pz.at[d - 1], at_z((z + d) % 4)) for d in range(1, 4)
    ]
    choose_rows()
    ring3(1, y_ring, yf)
    xf = x_swap(1)
    for g in range(32):
        k = (g % 2) * 16 + ((g // 4) % 4) * 4 + ((g // 2) % 2) * 2 + g // 16
        bsp[k * 8 : k * 8 + 8, :] = bs_ref[g * 8 : g * 8 + 8, :]

    for c in p2:
        c.wait_recv()
    pvb[core, z] += pz[0] + pz[1] + pz[2]
    p3 = [
        send(pvb.at[core, z, (x + d) % 4], px.at[d - 1], at_x((x + d) % 4)) for d in range(1, 4)
    ]
    x_add(1, xf)
    exchange()
    f1p.wait_recv()
    cb[core, zp, 0:2] += ru1[0]
    f2p = send(cb.at[core, zp], ru2.at[0], d_zp)
    f1m.wait_recv()
    cb[core, zm, 2:4] += ru1[1]
    f2m = send(cb.at[core, zm], ru2.at[1], d_zm)
    for c in p3:
        c.wait_recv()
    pb[col] = pvb[core, z, x] + px[0] + px[1] + px[2]
    p4 = [send(pb.at[col], pb.at[col], at_y((col + d) % 4)) for d in range(1, 4)]
    choose_ancestors()
    for c in p4:
        c.wait_recv()
    pfull[core, z, x] = pb[0] + pb[1] + pb[2] + pb[3]
    p5 = [
        send(pfull.at[core, z, x], pfull.at[core, z, x], at_x((x + d) % 4)) for d in range(1, 4)
    ]
    f2p.wait_recv()
    f2m.wait_recv()
    cb[core, z] += ru2[0] + ru2[1]
    rest = T - LEFT
    h1p = send(cb.at[core, z, x2, :, pl.ds(0, LEFT)], rv1.at[0], d_xp)
    h1m = send(cb.at[core, z, x2, :, pl.ds(LEFT, rest)], rv1.at[1, :, pl.ds(0, rest)], d_xm)
    for c in p5:
        c.wait_recv()
    p6 = [
        send(pfull.at[core, z], pfull.at[core, z], at_z((z + d) % 4)) for d in range(1, 4)
    ]
    h1p.wait_recv()
    cb[core, z, xp, :, :LEFT] += rv1[0]
    h2p = send(cb.at[core, z, xp], rv2.at[0], d_xp)
    h1m.wait_recv()
    cb[core, z, xm, :, LEFT:] += rv1[1, :, :rest]
    h2m = send(cb.at[core, z, xm], rv2.at[1], d_xm)
    for c in p6:
        c.wait_recv()
    p7 = send(pfull.at[core], pfull.at[core], d_core)

    pltpu.make_async_copy(got.at[pl.ds(0, DEV - 1)], got.at[pl.ds(0, DEV - 1)], arecv.at[0]).wait()
    received = got[...].reshape(8 * DEV, 128)
    both = jnp.concatenate([bs_ref[0:128, :], bs_ref[128:256, :]], 1)
    projected = three(received, both)
    first = (iota((8 * DEV, 128), 0) // 4) % 2 == 0
    projected = jnp.where(first, projected[:, :128], projected[:, 128:])
    charge = jnp.sum(ba8[...] * projected, 0, keepdims=True)
    h2p.wait_recv()
    h2m.wait_recv()
    upper_out[...] = cb[core, z, x] + rv2[0] + rv2[1]
    p7.wait_recv()
    pivot = pfull[...].reshape(S, S)
    charge_out[...] = charge + jnp.sum(bsp[...] * three(pivot, bs_ref[...]), 0, keepdims=True)
    pltpu.make_async_copy(pk.at[pl.ds(0, DEV - 1)], pk.at[pl.ds(0, DEV - 1)], asend.at[0]).wait()
    for c in started:
        c.wait_send()


N_COPIES = 80


def fused(weights, tile, lower, upper, pivot, owners, basis_super, basis_ancestor):
    vmem = pl.BlockSpec(memory_space=pltpu.VMEM)
    hbm = pl.BlockSpec(memory_space=pl.ANY)
    return pl.pallas_call(
        kernel,
        out_shape=(jax.ShapeDtypeStruct((8, T), F32), jax.ShapeDtypeStruct((1, 128), F32)),
        in_specs=[pl.BlockSpec(memory_space=pltpu.SMEM), hbm, hbm, hbm, vmem, vmem, vmem, hbm],
        out_specs=(vmem, vmem),
        scratch_shapes=[
            pltpu.VMEM((2, T, T), F32),
            pltpu.VMEM((2, T, T), BF16),
            pltpu.VMEM((2, T, T), BF16),
            pltpu.VMEM((4, 2, Q, T), F32),
            pltpu.VMEM((4, 2, Q, T), F32),
            pltpu.VMEM((2, Q, T), F32),
            pltpu.VMEM((4, S, T), BF16),
            pltpu.VMEM((4, S, T), BF16),
            pltpu.VMEM((2, S, T), BF16),
            pltpu.VMEM((2, S, T), BF16),
            pltpu.VMEM((2, T, 128), F32),
            pltpu.VMEM((2, T, 128), F32),
            pltpu.VMEM((T, S), BF16),
            pltpu.VMEM((T, S), BF16),
            pltpu.VMEM((T, S), BF16),
            pltpu.VMEM((T, S), BF16),
            pltpu.VMEM((S, T), F32),
            pltpu.VMEM((2, T, 128), F32),
            pltpu.VMEM((2, BLK, 128), F32),
            pltpu.VMEM((2, 2, BLK, 128), F32),
            pltpu.VMEM((2, SUB, 128), F32),
            pltpu.VMEM((2, 2, SUB, 128), F32),
            pltpu.VMEM((2, SUB, 128), F32),
            pltpu.VMEM((2, SUB, 128), F32),
            pltpu.VMEM((2, 4, 4, 8, T), F32),
            pltpu.VMEM((4, 4, 8, T), F32),
            pltpu.VMEM((2, 2, 8, T), F32),
            pltpu.VMEM((2, 4, 8, T), F32),
            pltpu.VMEM((2, 8, LEFT), F32),
            pltpu.VMEM((2, 8, T), F32),
            pltpu.VMEM((2, 4, 4, 8, S), F32),
            pltpu.VMEM((4, 4, 8, S), F32),
            pltpu.VMEM((3, 4, 8, S), F32),
            pltpu.VMEM((3, 8, S), F32),
            pltpu.VMEM((4, 8, S), F32),
            pltpu.VMEM((2, 4, 4, 8, S), F32),
            pltpu.VMEM((S, 128), F32),
            pltpu.VMEM((4608, 128), F32),
            pltpu.VMEM((8 * DEV, 128), F32),
            pltpu.VMEM((8 * DEV, 2 * SUB), BF16),
            pltpu.VMEM((DEV, 8, 128), F32),
            pltpu.VMEM((DEV, 8, 128), F32),
            pltpu.SemaphoreType.DMA((N_COPIES,)),
            pltpu.SemaphoreType.DMA((N_COPIES,)),
            pltpu.SemaphoreType.DMA((7,)),
            pltpu.SemaphoreType.DMA((1,)),
            pltpu.SemaphoreType.DMA((1,)),
        ],
        compiler_params=pltpu.CompilerParams(
            collective_id=0, has_side_effects=True, vmem_limit_bytes=63 << 20
        ),
    )(weights, tile, lower, upper, pivot, owners, basis_super, basis_ancestor)


def body(
    inverse_tile, lower_factor, upper_factor, pivot_inverse, pole_weights, block_owners,
    basis_ancestor, basis_super,
):
    owners = block_owners.T.reshape(TOPK, BAT, WIDE).transpose(1, 0, 2)
    upper_density, charge = fused(
        pole_weights, inverse_tile, lower_factor, upper_factor, pivot_inverse, owners, basis_super,
        basis_ancestor,
    )
    return (upper_density, charge.reshape(128))


def solution(mesh):
    placed = (
        P("pole", None, "row", "col"),
        P("pole", None, "row", "col"),
        P("pole", None, "col", "row"),
        P("pole", None, "row", "col"),
        P("pole", None),
        P(),
        P(None, ("pole", "row", "col")),
        P(None, ("pole", "row", "col")),
    )
    return jax.shard_map(
        body,
        mesh=mesh,
        in_specs=placed,
        out_specs=(P(("pole", "row"), "col"), P(("pole", "row", "col"))),
        check_vma=False,
    )
```

time: 113 us -> 80.7 us (0.71)
  waiting for transfers between devices: 14.1 us -> 0 us
  local copies, waits for them, and re-layouts: 14.2 us -> 4.19 us
  starting transfers between devices: 7.87 us -> 0 us
  Pallas kernels: 71 us -> 75.1 us
  matrix products: 2.65 us -> 0 us
    all_to_all x1 -> x0, waiting for transfers between devices: 14.1 us -> none  [body(): lax.all_to_all(packed, ('pole', 'row', 'col'), split_axis=0, concat_axis=...]
    all_to_all x1 -> x0, starting transfers between devices: 7.87 us -> none  [body(): lax.all_to_all(packed, ('pole', 'row', 'col'), split_axis=0, concat_axis=...]
    pallas_call x1, Pallas kernels: 71 us -> 75.1 us  [fused(): pl.pallas_call(kernel, out_shape=(jax.ShapeDtypeStruct((8, T), F32), jax....]
    dot_general x5 -> x0, matrix products: 2.65 us -> none  [the longest x1 1.5 us: body(): jnp.dot(received, basis_super, precision=high, preferred_element_type=F32)]
    slice x2 -> x0, local copies, waits for them, and re-layouts: 2.44 us -> none  [the longest x1 1.45 us: body(): pivot_density = got[:, 2].reshape(S, S)]
    dynamic_slice x2 -> x0, local copies, waits for them, and re-layouts: 1.74 us -> none  [the longest x1 0.93 us: body(): here = lax.dynamic_slice_in_dim(owners, group * NB, NB, 1)]
    gather x1 -> x0, local copies, waits for them, and re-layouts: 1.65 us -> none  [body(): ancestor_rows = jnp.take(basis_ancestor, row_ids, axis=0, mode='clip')]
    concatenate x1 -> x0, local copies, waits for them, and re-layouts: 1.53 us -> none  [body(): jnp.concatenate([packed, jnp.broadcast_to(pivot_part, (DEV, 1, 2 * S))], 1)]
  transfers between devices with their start and end apart: 1 -> 0, of which waited for: 1 -> 0; matrix products, arithmetic and copies ran while one was open for 3% -> 0% of each run, Pallas kernels for 0% -> 0%
where the time goes in v2:
time: 80.7 us; the launch traced here: 80 us
  Pallas kernels  75.1 us (93%)
  local copies, waits for them, and re-layouts  4.19 us (5%)
    pallas_call x1, Pallas kernels, fused(): pl.pallas_call(kernel, out_shape=(jax.ShapeDtypeStruct((8, T), F32), jax....  75.1 us
    unnamed x2, local copies, waits for them, and re-layouts  2.55 us
    reshape x2, local copies, waits for them, and re-layouts, body(): owners = block_owners.T.reshape(TOPK, BAT, WIDE).transpose(1, 0, 2)  1.64 us

profile of v2, /device:TPU:0, one launch (start us, length us, event | category | flops | bytes accessed | tf_op | source)
XLA Modules:
  0.0 80.0 jit_solution(13900695723107843284)
XLA Ops:
  0.6 1.0 %reshape.10 = s32[6,8,288]{2,1,0:T(8,128)S(1)} reshape(s32[6,2304]{1,0:T(8,128)} %bitcast.6) | data formatting | bytes 110592 | tf_op jit(solution)/shard_map/reshape | solution.py:598
  1.6 0.7 copy.12
  2.3 75.1 %shard_map.95 = (f32[8,1152]{1,0:T(8,128)}, f32[1,128]{1,0:T(1,128)}) custom-call(f32[1,2]{1,0:T(1,128)} %w_ref.1, f32[1,2,1152,1152]{3,2,1,0:T(8,128)} %a_hbm.1, f32[1,2,64,1152]{3,2,1,0:T(8,128)} %l_hbm.1, f32[1,2,64,1152]{3,2,1,0:T(8,128)} %u_hbm.1, f32[1,2,64,64]{3,2,1,0:T(8,128)} %piv_ref.1, s32[8,6,288]{2,1,0:T(8,128)} %bitcast.5, f32[256,128]{1,0:T(8,128)} %bs_ref.1, ...), custom_call_target="tpu_custom_call" | custom-call | tf_op jit(solution)/shard_map/pallas_call | solution.py:534
  77.4 1.4 %copy.15 = f32[8,1152]{1,0:T(8,128)} copy(f32[8,1152]{1,0:T(8,128)} %get-tuple-element.8) | data formatting | bytes 73728
  78.8 1.2 %copy.16 = f32[128]{0:T(128)} copy(f32[128]{0:T(128)} %bitcast.7) | data formatting | bytes 1024

commit v3 on v2

--- a/solution.py
+++ b/solution.py
@@ -20,6 +20,7 @@
 BLK = 288
 SUB = 72
 FIRST = 40
+TAIL = 1024
 LEFT = 640
 
 
@@ -50,10 +51,10 @@
 
 def kernel(
     w_ref, a_hbm, l_hbm, u_hbm, piv_ref, own_ref, bs_ref, ba_hbm,
-    upper_out, charge_out,
+    out_ref,
     a32, ah, al, lf, uf, relay, bl, br, uph, upl, xr, xi, xih, xil, xrh, xrl, y, lt,
     rz1, rz2, ry1, ry2, rx, ld, cb, rc, ru1, ru2, rv1, rv2,
-    pvb, pc, pz, px, pb, pfull, bsp, ba, ba8, sel, pk, got,
+    pvb, pc, pz, pb, pfull, bsp, ba, ba8, sel, pk, got, own_s, pvs, ath, atl, bt,
     sends, recvs, locs, asend, arecv,
 ):
     pole, row, col = lax.axis_index("pole"), lax.axis_index("row"), lax.axis_index("col")
@@ -104,13 +105,27 @@
     local_u = pltpu.make_async_copy(u_hbm.at[0], uf.at[col], locs.at[5])
     local_ba = pltpu.make_async_copy(ba_hbm, ba, locs.at[6])
     local_l.start()
-    local_a[0].start()
-    local_a[1].start()
+    for c in local_a:
+        c.start()
+
+    def split_a(b):
+        local_a[b].wait()
+
+        @pl.loop(0, BLK // 16)
+        def _(i):
+            rs = pl.ds(pl.multiple_of(b * BLK + i * 16, 16), 16)
+            for part in range(2):
+                hi, low = split(a32[part, rs, :])
+                ah[part, rs, :] = hi
+                al[part, rs, :] = low
+                ath[rs, part * 128 : part * 128 + 128] = hi[:, TAIL:]
+                atl[rs, part * 128 : part * 128 + 128] = low[:, TAIL:]
 
     barrier = pltpu.get_barrier_semaphore()
-    greet = (d_core, d_xp, d_xm, at_x(x2), d_yp, d_ym, at_y(y2), d_zp, d_zm, at_z(z2))
+    greet = (d_core, d_xp, d_xm, d_yp, d_ym, d_zp, d_zm)
     for dev in greet:
         pl.semaphore_signal(barrier, inc=1, device_id=dev, device_id_type=MESH)
+    split_a(0)
     pl.semaphore_wait(barrier, len(greet))
 
     def lanes(k):
@@ -149,15 +164,13 @@
         m = send(uf.at[yp, 1, :, lanes(k)], uf.at[yp, 1, :, lanes(k)], d_ym)
         return p, m
 
-    l_near = send(l_hbm.at[0], lf.at[row], d_core)
-    lo = [l_own(0)]
-    uo = [u_own(0)]
-    lo.append(l_own(1))
-    uo.append(u_own(1))
-    local_a[2].start()
-    local_a[3].start()
+    l_near, lo, uo = [], [], []
+    for k in range(3):
+        l_near.append(send(l_hbm.at[0, :, :, lanes(k)], lf.at[row, :, :, lanes(k)], d_core))
+        lo.append(l_own(k))
+        uo.append(u_own(k))
+    local_ba.start()
     local_u.start()
-    local_ba.start()
 
     w_re, w_im = w_ref[0, 0], w_ref[0, 1]
 
@@ -166,6 +179,13 @@
         a, b = pl.ds(q * Q, Q), pl.ds(2 * Q + q * Q, Q)
         rh, rl = split(re)
         ih, il = split(im)
+        if lane.start == TAIL:
+            one, two = pl.ds(0, 128), pl.ds(128, 128)
+            bt[0, a, one], bt[1, a, one] = rh, rl
+            bt[0, b, one], bt[1, b, one] = ih, il
+            bt[0, a, two], bt[1, a, two] = -ih, -il
+            bt[0, b, two], bt[1, b, two] = rh, rl
+            return
         dst[0, a, lane], dst[1, a, lane] = rh, rl
         dst[0, b, lane], dst[1, b, lane] = ih, il
         dst[2, a, lane], dst[3, a, lane] = -ih, -il
@@ -179,25 +199,6 @@
         acc = acc + nt(ah[1, rs, lane], b[3, :, lane])
         acc = acc + nt(al[1, rs, lane], b[2, :, lane])
         return acc
-
-    def split_a(b):
-        local_a[b].wait()
-
-        @pl.loop(0, BLK // 16)
-        def _(i):
-            rs = pl.ds(pl.multiple_of(b * BLK + i * 16, 16), 16)
-            for part in range(2):
-                hi, low = split(a32[part, rs, :])
-                ah[part, rs, :] = hi
-                al[part, rs, :] = low
-
-    whole = pl.ds(0, T)
-
-    def near(b):
-        rs = pl.ds(b * BLK, BLK)
-        acc = product(rs, whole, bl)
-        xr[x_hi, rs, :] = acc[:, :128]
-        xi[x_hi, rs, :] = acc[:, 128:]
 
     halves = (x_hi, 1 - x_hi)
 
@@ -252,7 +253,7 @@
         before.wait_recv()
         ld[halves[n]] = lt[halves[n], rows_of(y_at(col), SUB), :] + rx[n]
 
-    def upper_chunk(k):
+    def upper_prep(k):
         lane = lanes(k)
         for q in range(4):
             re, im = uf[q, 0, :, lane], uf[q, 1, :, lane]
@@ -261,6 +262,9 @@
                 hi, low = split(v)
                 uph[part, rs, lane] = hi
                 upl[part, rs, lane] = low
+
+    def upper_chunk(k):
+        lane = lanes(k)
         acc = nn(uph[0, :, lane], ah[1, lane, :])
         acc = acc + nn(uph[0, :, lane], al[1, lane, :])
         acc = acc + nn(upl[0, :, lane], ah[1, lane, :])
@@ -272,23 +276,43 @@
         else:
             y[...] += acc
 
-    def far_chunk(k):
-        for q in range(2):
-            build(br, (1 - x_hi) * 2 + q, q, lanes(k))
-
-        @pl.loop(0, 4)
+    def chunk(n, k, blocks=(0, 4)):
+        dst, h = ((bl, br)[n], halves[n])
+        if blocks[0] == 0:
+            for q in range(2):
+                build(dst, h * 2 + q, q, lanes(k))
+
+        @pl.loop(*blocks)
         def _(b):
             rs = pl.ds(pl.multiple_of(b * BLK, 16), BLK)
-            acc = product(rs, lanes(k), br)
+            if k == 2:
+                acc = nt(ath[rs, :], bt[0]) + nt(ath[rs, :], bt[1]) + nt(atl[rs, :], bt[0])
+            else:
+                acc = product(rs, lanes(k), dst)
             if k == 0:
-                xr[1 - x_hi, rs, :] = acc[:, :128]
-                xi[1 - x_hi, rs, :] = acc[:, 128:]
+                xr[h, rs, :] = acc[:, :128]
+                xi[h, rs, :] = acc[:, 128:]
             else:
-                xr[1 - x_hi, rs, :] += acc[:, :128]
-                xi[1 - x_hi, rs, :] += acc[:, 128:]
+                xr[h, rs, :] += acc[:, :128]
+                xi[h, rs, :] += acc[:, 128:]
+
+    def pivot_chunk(k):
+        lane = lanes(k)
+        acc = nn(uph[0, :, lane], xih[lane, :])
+        acc = acc + nn(uph[0, :, lane], xil[lane, :])
+        acc = acc + nn(upl[0, :, lane], xih[lane, :])
+        acc = acc + nn(uph[1, :, lane], xrh[lane, :])
+        acc = acc + nn(uph[1, :, lane], xrl[lane, :])
+        acc = acc + nn(upl[1, :, lane], xrh[lane, :])
+        if k == 0:
+            pvs[...] = acc
+        else:
+            pvs[...] += acc
 
     def choose_rows():
-        mine = own_ref[group // 16].astype(F32).astype(BF16)
+        for b in range(BAT):
+            own_s[b] = own_ref[:, b * WIDE : (b + 1) * WIDE]
+        mine = own_s[group // 16].astype(F32).astype(BF16)
         here = nn(
             mine,
             (iota((WIDE, NB), 0) == (group % 16) * NB + iota((WIDE, NB), 1)).astype(F32).astype(BF16),
@@ -313,17 +337,18 @@
         keep = ((ro // 4) % 2 == co // SUB) & (ro % 2 == co % 2)
         sel[...] = jnp.where(keep, full, 0.0).astype(BF16)
 
-    def choose_ancestors():
-        local_ba.wait()
+    def choose_ancestors(start, stop):
+        if start == 0:
+            local_ba.wait()
         block = iota((WIDE, WIDE), 0), iota((WIDE, WIDE), 1)
         earlier = ((block[0] // NB == block[1] // NB) & (block[0] < block[1])).astype(F32)
         earlier = earlier.astype(BF16)
         slot = iota((8 * 16, WIDE), 0)
         wanted = slot - (slot // 4) % 2 * 4 - slot % 2
 
-        @pl.loop(0, BAT)
+        @pl.loop(start, stop)
         def _(b):
-            owners = own_ref[b]
+            owners = own_s[b]
             mine = jnp.max((owners == me).astype(F32), 0, keepdims=True)
             rank = nn(jnp.broadcast_to(mine, (8, WIDE)).astype(BF16), earlier)[0:1, :]
             base = (iota((1, WIDE), 1) // NB * 8).astype(F32)
@@ -345,12 +370,12 @@
         pk[...] = packed.reshape(DEV, 8, 128)
         got[group] = pk[me]
 
-        @pl.loop(1, DEV)
-        def _(d):
-            t = (me + d) % DEV
+        for n in range(1, DEV):
+            p, r, c = (pole + n // 16) % 8, (row + n // 4) % 4, (col + n) % 4
             pltpu.make_async_remote_copy(
-                src_ref=pk.at[t], dst_ref=got.at[group], send_sem=asend.at[0], recv_sem=arecv.at[0],
-                device_id=(t // 16, (t // 4) % 4, t % 4), device_id_type=MESH,
+                src_ref=pk.at[(p * 4 + r) * 4 + c], dst_ref=got.at[group],
+                send_sem=asend.at[0], recv_sem=arecv.at[0],
+                device_id=(p, r, c), device_id_type=MESH,
             ).start()
 
     def three(a, b):
@@ -358,40 +383,40 @@
         bhi, blo = split(b)
         return nn(ahi, bhi) + nn(ahi, blo) + nn(alo, bhi)
 
+    for b in range(1, 4):
+        split_a(b)
     local_l.wait()
-    l_near.wait_recv()
-    for q in range(2):
-        build(bl, x_hi * 2 + q, q, whole)
-    split_a(0)
-    near(0)
-    split_a(1)
+    l_near[0].wait_recv()
+    chunk(0, 0)
+    l_near[1].wait_recv()
+    chunk(0, 1, (0, 2))
     lr = [l_relay(0, lo[0])]
-    lo.append(l_own(2))
-    near(1)
-    split_a(2)
-    lr.append(l_relay(1, lo[1]))
-    uf_moves = [u_forward(0, uo[0])]
-    uo.append(u_own(2))
-    near(2)
-    ls = [l_share(0, lr[0])]
-    lr.append(l_relay(2, lo[2]))
-    split_a(3)
-    near(3)
+    chunk(0, 1, (2, 4))
+    l_near[2].wait_recv()
+    chunk(0, 2)
     lower_term(0)
     zn = ring1(0, z_ring)
+    lr.append(l_relay(1, lo[1]))
+    lr.append(l_relay(2, lo[2]))
+    uf_moves = [u_forward(0, uo[0])]
+    choose_rows()
+    choose_ancestors(0, 4)
+    ls = [l_share(0, lr[0])]
+    choose_ancestors(4, 8)
+    zn = ring2(0, z_ring, zn)
+    ls[0].wait_recv()
+    chunk(1, 0, (0, 2))
     ls.append(l_share(1, lr[1]))
-    ls[0].wait_recv()
-    far_chunk(0)
-    zn = ring2(0, z_ring, zn)
     uf_moves.append(u_forward(1, uo[1]))
+    chunk(1, 0, (2, 4))
     ls.append(l_share(2, lr[2]))
+    uf_moves.append(u_forward(2, uo[2]))
     ls[1].wait_recv()
-    far_chunk(1)
-    uf_moves.append(u_forward(2, uo[2]))
+    chunk(1, 1)
     ring3(0, z_ring, zn)
     yn = ring1(0, y_ring)
     ls[2].wait_recv()
-    far_chunk(2)
+    chunk(1, 2)
     lower_term(1)
     zf = ring1(1, z_ring)
     local_u.wait()
@@ -403,32 +428,23 @@
         xrh[:, hs], xrl[:, hs] = hi, low
     for c in uf_moves[0]:
         c.wait_recv()
+    upper_prep(0)
+    upper_chunk(0)
+    yn = ring2(0, y_ring, yn)
+    pivot_chunk(0)
     zf = ring2(1, z_ring, zf)
-    yn = ring2(0, y_ring, yn)
-    upper_chunk(0)
+    for c in uf_moves[1]:
+        c.wait_recv()
+    upper_prep(1)
+    upper_chunk(1)
     ring3(0, y_ring, yn)
     xn = x_swap(0)
-    for c in uf_moves[1]:
-        c.wait_recv()
-    upper_chunk(1)
-    ring3(1, z_ring, zf)
-    yf = ring1(1, y_ring)
-    x_add(0, xn)
+    pivot_chunk(1)
     for c in uf_moves[2]:
         c.wait_recv()
-    upper_chunk(2)
-
-    for g in range(32):
-        at = (g % 2, (g // 4) % 4, ((g // 2) % 2) * 2 + g // 16)
-        cb[at[0], at[1], at[2]] = -y[g * 8 : g * 8 + 8, :]
-    to_core = send(cb.at[1 - core], rc, d_core)
-
-    pv = nn(uph[0], xih[...])
-    pv = pv + nn(uph[0], xil[...])
-    pv = pv + nn(upl[0], xih[...])
-    pv = pv + nn(uph[1], xrh[...])
-    pv = pv + nn(uph[1], xrl[...])
-    pv = pv + nn(upl[1], xrh[...])
+    upper_prep(2)
+    pivot_chunk(2)
+
     place = (iota((Q, S), 1) == iota((Q, S), 0) + col * Q).astype(F32)
     piece = w_re * piv_ref[0, 1] + w_im * piv_ref[0, 0]
     placed = jnp.dot(piece, place, precision=lax.Precision.HIGHEST, preferred_element_type=F32)
@@ -436,11 +452,29 @@
         at = (g % 2, (g // 4) % 4, ((g // 2) % 2) * 2 + g // 16)
         mine = (row == g // 8).astype(F32)
         pvb[at[0], at[1], at[2]] = (
-            pv[g * 8 : g * 8 + 8, :] + mine * placed[(g % 8) * 8 : (g % 8) * 8 + 8, :]
+            pvs[g * 8 : g * 8 + 8, :] + mine * placed[(g % 8) * 8 : (g % 8) * 8 + 8, :]
         )
     p1 = send(pvb.at[1 - core], pc, d_core)
-    yf = ring2(1, y_ring, yf)
-
+    upper_chunk(2)
+    for g in range(32):
+        at = (g % 2, (g // 4) % 4, ((g // 2) % 2) * 2 + g // 16)
+        cb[at[0], at[1], at[2]] = -y[g * 8 : g * 8 + 8, :]
+    to_core = send(cb.at[1 - core], rc, d_core)
+    ring3(1, z_ring, zf)
+    yf = ring1(1, y_ring)
+    p1.wait_recv()
+    pvb[core] += pc[...]
+
+    def in_plane(n, other):
+        zz, xx = (z + n // 4) % 4, (x + n) % 4
+        cc = (core + other) % 2
+        return zz, xx, ((xx % 2) * 4 + zz, (xx // 2) * 2 + cc, col)
+
+    p2 = []
+    for n in range(1, 16):
+        zz, xx, dev = in_plane(n, 0)
+        p2.append(send(pvb.at[core, zz, xx], pz.at[n - 1], dev))
+    x_add(0, xn)
     to_core.wait_recv()
 
     @pl.loop(0, 4)
@@ -449,63 +483,47 @@
 
     f1p = send(cb.at[core, z2, pl.ds(0, 2)], ru1.at[0], d_zp)
     f1m = send(cb.at[core, z2, pl.ds(2, 2)], ru1.at[1], d_zm)
-    p1.wait_recv()
-    pvb[core] += pc[...]
-    p2 = [
-        send(pvb.at[core, (z + d) % 4], pz.at[d - 1], at_z((z + d) % 4)) for d in range(1, 4)
-    ]
-    choose_rows()
-    ring3(1, y_ring, yf)
-    xf = x_swap(1)
+    yf = ring2(1, y_ring, yf)
     for g in range(32):
         k = (g % 2) * 16 + ((g // 4) % 4) * 4 + ((g // 2) % 2) * 2 + g // 16
         bsp[k * 8 : k * 8 + 8, :] = bs_ref[g * 8 : g * 8 + 8, :]
-
     for c in p2:
         c.wait_recv()
-    pvb[core, z] += pz[0] + pz[1] + pz[2]
-    p3 = [
-        send(pvb.at[core, z, (x + d) % 4], px.at[d - 1], at_x((x + d) % 4)) for d in range(1, 4)
-    ]
-    x_add(1, xf)
-    exchange()
+    pb[col] = pvb[core, z, x] + jnp.sum(pz[...], 0)
+    p4 = [send(pb.at[col], pb.at[col], at_y((col + d) % 4)) for d in range(1, 4)]
+    ring3(1, y_ring, yf)
+    xf = x_swap(1)
     f1p.wait_recv()
     cb[core, zp, 0:2] += ru1[0]
     f2p = send(cb.at[core, zp], ru2.at[0], d_zp)
     f1m.wait_recv()
     cb[core, zm, 2:4] += ru1[1]
     f2m = send(cb.at[core, zm], ru2.at[1], d_zm)
-    for c in p3:
-        c.wait_recv()
-    pb[col] = pvb[core, z, x] + px[0] + px[1] + px[2]
-    p4 = [send(pb.at[col], pb.at[col], at_y((col + d) % 4)) for d in range(1, 4)]
-    choose_ancestors()
     for c in p4:
         c.wait_recv()
     pfull[core, z, x] = pb[0] + pb[1] + pb[2] + pb[3]
-    p5 = [
-        send(pfull.at[core, z, x], pfull.at[core, z, x], at_x((x + d) % 4)) for d in range(1, 4)
-    ]
+    p5 = []
+    for n in range(1, 32):
+        zz, xx, dev = in_plane(n // 2, n % 2)
+        p5.append(send(pfull.at[core, z, x], pfull.at[core, z, x], dev))
+    x_add(1, xf)
+    exchange()
     f2p.wait_recv()
     f2m.wait_recv()
     cb[core, z] += ru2[0] + ru2[1]
     rest = T - LEFT
     h1p = send(cb.at[core, z, x2, :, pl.ds(0, LEFT)], rv1.at[0], d_xp)
     h1m = send(cb.at[core, z, x2, :, pl.ds(LEFT, rest)], rv1.at[1, :, pl.ds(0, rest)], d_xm)
-    for c in p5:
-        c.wait_recv()
-    p6 = [
-        send(pfull.at[core, z], pfull.at[core, z], at_z((z + d) % 4)) for d in range(1, 4)
-    ]
     h1p.wait_recv()
     cb[core, z, xp, :, :LEFT] += rv1[0]
     h2p = send(cb.at[core, z, xp], rv2.at[0], d_xp)
     h1m.wait_recv()
     cb[core, z, xm, :, LEFT:] += rv1[1, :, :rest]
     h2m = send(cb.at[core, z, xm], rv2.at[1], d_xm)
-    for c in p6:
+    for c in p5:
         c.wait_recv()
-    p7 = send(pfull.at[core], pfull.at[core], d_core)
+    pivot = pfull[...].reshape(S, S)
+    charge = jnp.sum(bsp[...] * three(pivot, bs_ref[...]), 0, keepdims=True)
 
     pltpu.make_async_copy(got.at[pl.ds(0, DEV - 1)], got.at[pl.ds(0, DEV - 1)], arecv.at[0]).wait()
     received = got[...].reshape(8 * DEV, 128)
@@ -513,19 +531,17 @@
     projected = three(received, both)
     first = (iota((8 * DEV, 128), 0) // 4) % 2 == 0
     projected = jnp.where(first, projected[:, :128], projected[:, 128:])
-    charge = jnp.sum(ba8[...] * projected, 0, keepdims=True)
+    charge = charge + jnp.sum(ba8[...] * projected, 0, keepdims=True)
     h2p.wait_recv()
     h2m.wait_recv()
-    upper_out[...] = cb[core, z, x] + rv2[0] + rv2[1]
-    p7.wait_recv()
-    pivot = pfull[...].reshape(S, S)
-    charge_out[...] = charge + jnp.sum(bsp[...] * three(pivot, bs_ref[...]), 0, keepdims=True)
+    out_ref[:, :T] = cb[core, z, x] + rv2[0] + rv2[1]
+    out_ref[:, T:] = jnp.broadcast_to(charge, (8, 128))
     pltpu.make_async_copy(pk.at[pl.ds(0, DEV - 1)], pk.at[pl.ds(0, DEV - 1)], asend.at[0]).wait()
     for c in started:
         c.wait_send()
 
 
-N_COPIES = 80
+N_COPIES = 112
 
 
 def fused(weights, tile, lower, upper, pivot, owners, basis_super, basis_ancestor):
@@ -533,9 +549,9 @@
     hbm = pl.BlockSpec(memory_space=pl.ANY)
     return pl.pallas_call(
         kernel,
-        out_shape=(jax.ShapeDtypeStruct((8, T), F32), jax.ShapeDtypeStruct((1, 128), F32)),
+        out_shape=jax.ShapeDtypeStruct((8, T + 128), F32),
         in_specs=[pl.BlockSpec(memory_space=pltpu.SMEM), hbm, hbm, hbm, vmem, vmem, vmem, hbm],
-        out_specs=(vmem, vmem),
+        out_specs=vmem,
         scratch_shapes=[
             pltpu.VMEM((2, T, T), F32),
             pltpu.VMEM((2, T, T), BF16),
@@ -569,8 +585,7 @@
             pltpu.VMEM((2, 8, T), F32),
             pltpu.VMEM((2, 4, 4, 8, S), F32),
             pltpu.VMEM((4, 4, 8, S), F32),
-            pltpu.VMEM((3, 4, 8, S), F32),
-            pltpu.VMEM((3, 8, S), F32),
+            pltpu.VMEM((15, 8, S), F32),
             pltpu.VMEM((4, 8, S), F32),
             pltpu.VMEM((2, 4, 4, 8, S), F32),
             pltpu.VMEM((S, 128), F32),
@@ -579,6 +594,11 @@
             pltpu.VMEM((8 * DEV, 2 * SUB), BF16),
             pltpu.VMEM((DEV, 8, 128), F32),
             pltpu.VMEM((DEV, 8, 128), F32),
+            pltpu.VMEM((BAT, TOPK, WIDE), jnp.int32),
+            pltpu.VMEM((S, S), F32),
+            pltpu.VMEM((T, S), BF16),
+            pltpu.VMEM((T, S), BF16),
+            pltpu.VMEM((2, S, S), BF16),
             pltpu.SemaphoreType.DMA((N_COPIES,)),
             pltpu.SemaphoreType.DMA((N_COPIES,)),
             pltpu.SemaphoreType.DMA((7,)),
@@ -595,12 +615,11 @@
     inverse_tile, lower_factor, upper_factor, pivot_inverse, pole_weights, block_owners,
     basis_ancestor, basis_super,
 ):
-    owners = block_owners.T.reshape(TOPK, BAT, WIDE).transpose(1, 0, 2)
-    upper_density, charge = fused(
-        pole_weights, inverse_tile, lower_factor, upper_factor, pivot_inverse, owners, basis_super,
-        basis_ancestor,
+    out = fused(
+        pole_weights, inverse_tile, lower_factor, upper_factor, pivot_inverse, block_owners.T,
+        basis_super, basis_ancestor,
     )
-    return (upper_density, charge.reshape(128))
+    return (out[:, :T], out[0, T:])
 
 
 def solution(mesh):

time: 80.7 us -> 68.9 us (0.85)
  Pallas kernels: 75.1 us -> 65.5 us
  local copies, waits for them, and re-layouts: 4.19 us -> 2.57 us
    pallas_call x1, Pallas kernels: 75.1 us -> 65.5 us  [fused(): pl.pallas_call(kernel, out_shape=jax.ShapeDtypeStruct((8, T + 128), F32),...]
    unnamed x2 -> x0, local copies, waits for them, and re-layouts: 2.55 us -> none
    reshape x2 -> x0, local copies, waits for them, and re-layouts: 1.64 us -> none  [body(): owners = block_owners.T.reshape(TOPK, BAT, WIDE).transpose(1, 0, 2)]
    slice x0 -> x1, local copies, waits for them, and re-layouts: none -> 1.39 us  [body(): return (out[:, :T], out[0, T:])]
    squeeze x0 -> x1, local copies, waits for them, and re-layouts: none -> 1.19 us  [body(): return (out[:, :T], out[0, T:])]
where the time goes in v3:
time: 68.9 us; the launch traced here: 68.7 us
  Pallas kernels  65.5 us (95%)
  local copies, waits for them, and re-layouts  2.57 us (4%)
    pallas_call x1, Pallas kernels, fused(): pl.pallas_call(kernel, out_shape=jax.ShapeDtypeStruct((8, T + 128), F32),...  65.5 us
    slice x1, local copies, waits for them, and re-layouts, body(): return (out[:, :T], out[0, T:])  1.39 us

profile of v3, /device:TPU:0, one launch (start us, length us, event | category | flops | bytes accessed | tf_op | source)
XLA Modules:
  0.0 68.7 jit_solution(10929175826290051729)
XLA Ops:
  0.6 65.5 %shard_map.95 = f32[8,1280]{1,0:T(8,128)} custom-call(f32[1,2]{1,0:T(1,128)} %w_ref.1, f32[1,2,1152,1152]{3,2,1,0:T(8,128)} %a_hbm.1, f32[1,2,64,1152]{3,2,1,0:T(8,128)} %l_hbm.1, f32[1,2,64,1152]{3,2,1,0:T(8,128)} %u_hbm.1, f32[1,2,64,64]{3,2,1,0:T(8,128)} %piv_ref.1, s32[6,2304]{1,0:T(8,128)} %bitcast.3, f32[256,128]{1,0:T(8,128)} %bs_ref.1, ...), custom_call_target="tpu_custom_call" | custom-call | tf_op jit(solution)/shard_map/pallas_call | solution.py:550
  66.1 1.2 %slice_bitcast_fusion = f32[128]{0:T(128)} fusion(f32[8,1280]{1,0:T(8,128)} %shard_map.95), kind=kLoop, calls=%fused_computation | loop fusion | bytes 1024 | tf_op jit(solution)/shard_map/squeeze | solution.py:622
  67.3 1.4 %slice.6 = f32[8,1152]{1,0:T(8,128)} slice(f32[8,1280]{1,0:T(8,128)} %shard_map.95), slice={[0:8], [0:1152]} | slice | bytes 73728 | tf_op jit(solution)/shard_map/slice | solution.py:622

commit v4 on v3

--- a/solution.py
+++ b/solution.py
@@ -19,9 +19,7 @@
 CHUNKS = ((0, 512), (512, 512), (1024, 128))
 BLK = 288
 SUB = 72
-FIRST = 40
 TAIL = 1024
-LEFT = 640
 
 
 def nt(a, b):
@@ -52,9 +50,9 @@
 def kernel(
     w_ref, a_hbm, l_hbm, u_hbm, piv_ref, own_ref, bs_ref, ba_hbm,
     out_ref,
-    a32, ah, al, lf, uf, relay, bl, br, uph, upl, xr, xi, xih, xil, xrh, xrl, y, lt,
-    rz1, rz2, ry1, ry2, rx, ld, cb, rc, ru1, ru2, rv1, rv2,
-    pvb, pc, pz, pb, pfull, bsp, ba, ba8, sel, pk, got, own_s, pvs, ath, atl, bt,
+    a32, ah, al, lf, uf, bl, br, uph, upl, xr, xi, xih, xil, xrh, xrl, y, lt,
+    rz1, rz2, ry, rx, ld, cb, rc, ru1, ru2, rv,
+    pvb, pc, pz, pb, pfull, bsp, ba, ba4, sel, pk, got, own_s, pvs, ath, atl, bt,
     sends, recvs, locs, asend, arecv,
 ):
     pole, row, col = lax.axis_index("pole"), lax.axis_index("row"), lax.axis_index("col")
@@ -122,7 +120,7 @@
                 atl[rs, part * 128 : part * 128 + 128] = low[:, TAIL:]
 
     barrier = pltpu.get_barrier_semaphore()
-    greet = (d_core, d_xp, d_xm, d_yp, d_ym, d_zp, d_zm)
+    greet = (d_core, d_xp, d_xm, at_x(x2), d_yp, d_ym, d_zp, d_zm)
     for dev in greet:
         pl.semaphore_signal(barrier, inc=1, device_id=dev, device_id_type=MESH)
     split_a(0)
@@ -132,23 +130,12 @@
         return pl.ds(CHUNKS[k][0], CHUNKS[k][1])
 
     def l_own(k):
-        return (
-            send(l_hbm.at[0, 0, :, lanes(k)], relay.at[0, :, lanes(k)], d_xp),
-            send(l_hbm.at[0, 1, :, lanes(k)], relay.at[1, :, lanes(k)], d_xm),
-        )
-
-    def l_relay(k, own):
-        own[0].wait_recv()
-        p = send(relay.at[0, :, lanes(k)], lf.at[row_x(xm), 0, :, lanes(k)], d_xp)
-        own[1].wait_recv()
-        m = send(relay.at[1, :, lanes(k)], lf.at[row_x(xp), 1, :, lanes(k)], d_xm)
-        return p, m
+        return send(l_hbm.at[0, :, :, lanes(k)], lf.at[row, :, :, lanes(k)], at_x(x2))
 
     far = (1 - x_hi) * 2 + core
 
-    def l_share(k, pair):
-        pair[0].wait_recv()
-        pair[1].wait_recv()
+    def l_share(k, own):
+        own.wait_recv()
         return send(lf.at[far, :, :, lanes(k)], lf.at[far, :, :, lanes(k)], d_core)
 
     def u_own(k):
@@ -217,7 +204,18 @@
         return z * BLK + b * SUB
 
     z_ring = (z_at, BLK, 144, (zp, zm, z2, z), (d_zp, d_zm), rz1, rz2)
-    y_ring = (y_at, SUB, FIRST, (yp, ym, y2, col), (d_yp, d_ym), ry1, ry2)
+
+    def y_send(n):
+        h = halves[n]
+        return [
+            send(lt.at[h, rows_of(y_at((col + d) % 4), SUB), :], ry.at[n, d - 1], at_y((col + d) % 4))
+            for d in range(1, 4)
+        ]
+
+    def y_sum(n, before):
+        for c in before:
+            c.wait_recv()
+        lt[halves[n], rows_of(y_at(col), SUB), :] += ry[n, 0] + ry[n, 1] + ry[n, 2]
 
     def ring1(n, ring):
         at, size, first, (p, m, two, own), (dp, dm), r1, r2 = ring
@@ -325,16 +323,15 @@
         earlier = (iota((NB, NB), 0) < iota((NB, NB), 1)).astype(F32).astype(BF16)
         rank = nn(named.astype(BF16), earlier)
         chosen = named * (rank == (owner % 2).astype(F32)).astype(F32)
-        spot = iota((NB, 2 * SUB), 1) % SUB
+        spot = iota((NB, SUB), 1)
         spread = (
-            (spot // 36 == x_lo) & ((spot % 36) // 2 == iota((NB, 2 * SUB), 0))
+            (spot // 36 == x_lo) & ((spot % 36) // 2 == iota((NB, SUB), 0))
         ).astype(F32)
         wide = nn(chosen.astype(BF16), spread.astype(BF16))
-        out = iota((8 * DEV, 2 * DEV), 0)
-        repeat = (iota((8 * DEV, 2 * DEV), 1) == (out // 8) * 2 + (out // 2) % 2).astype(F32)
+        out = iota((4 * DEV, 2 * DEV), 0)
+        repeat = (iota((4 * DEV, 2 * DEV), 1) == out // 2).astype(F32)
         full = nn(repeat.astype(BF16), wide.astype(BF16))
-        ro, co = iota((8 * DEV, 2 * SUB), 0), iota((8 * DEV, 2 * SUB), 1)
-        keep = ((ro // 4) % 2 == co // SUB) & (ro % 2 == co % 2)
+        keep = iota((4 * DEV, SUB), 0) % 2 == iota((4 * DEV, SUB), 1) % 2
         sel[...] = jnp.where(keep, full, 0.0).astype(BF16)
 
     def choose_ancestors(start, stop):
@@ -343,38 +340,38 @@
         block = iota((WIDE, WIDE), 0), iota((WIDE, WIDE), 1)
         earlier = ((block[0] // NB == block[1] // NB) & (block[0] < block[1])).astype(F32)
         earlier = earlier.astype(BF16)
-        slot = iota((8 * 16, WIDE), 0)
-        wanted = slot - (slot // 4) % 2 * 4 - slot % 2
+        slot = iota((4 * 16, WIDE), 0)
+        wanted = slot - slot % 2
 
         @pl.loop(start, stop)
         def _(b):
             owners = own_s[b]
             mine = jnp.max((owners == me).astype(F32), 0, keepdims=True)
             rank = nn(jnp.broadcast_to(mine, (8, WIDE)).astype(BF16), earlier)[0:1, :]
-            base = (iota((1, WIDE), 1) // NB * 8).astype(F32)
+            base = (iota((1, WIDE), 1) // NB * 4).astype(F32)
             key = jnp.where(mine > 0, base + 2 * rank, -8.0)
             hit = key == wanted.astype(F32)
-            acc = jnp.zeros((8 * 16, 128), F32)
+            acc = jnp.zeros((4 * 16, 128), F32)
             for parity in range(2):
                 one = (hit & (slot % 2 == parity)).astype(F32).astype(BF16)
                 v = ba[pl.ds(b * 2 * WIDE + parity, WIDE, stride=2), :]
                 hi, low = split(v)
                 acc = acc + nn(one, hi) + nn(one, low)
-            ba8[rows_of(b * 128, 128), :] = acc
-
-    def exchange():
-        v = ld[...].reshape(2 * SUB, 128)
+            ba4[rows_of(b * 64, 64), :] = acc
+
+    def exchange(n):
+        h = halves[n]
+        v = ld[h]
         hi, low = split(v)
         rest = (v - hi.astype(F32) - low.astype(F32)).astype(BF16)
         packed = nn(sel[...], hi) + nn(sel[...], low) + nn(sel[...], rest)
-        pk[...] = packed.reshape(DEV, 8, 128)
-        got[group] = pk[me]
-
-        for n in range(1, DEV):
-            p, r, c = (pole + n // 16) % 8, (row + n // 4) % 4, (col + n) % 4
+        pk[n] = packed.reshape(DEV, 4, 128)
+        got[h, group] = pk[n, me]
+        for i in range(1, DEV):
+            p, r, c = (pole + i // 16) % 8, (row + i // 4) % 4, (col + i) % 4
             pltpu.make_async_remote_copy(
-                src_ref=pk.at[(p * 4 + r) * 4 + c], dst_ref=got.at[group],
-                send_sem=asend.at[0], recv_sem=arecv.at[0],
+                src_ref=pk.at[n, (p * 4 + r) * 4 + c], dst_ref=got.at[h, group],
+                send_sem=asend.at[n], recv_sem=arecv.at[h],
                 device_id=(p, r, c), device_id_type=MESH,
             ).start()
 
@@ -389,37 +386,34 @@
     l_near[0].wait_recv()
     chunk(0, 0)
     l_near[1].wait_recv()
-    chunk(0, 1, (0, 2))
-    lr = [l_relay(0, lo[0])]
-    chunk(0, 1, (2, 4))
+    chunk(0, 1)
     l_near[2].wait_recv()
     chunk(0, 2)
+    ls = [l_share(0, lo[0])]
     lower_term(0)
     zn = ring1(0, z_ring)
-    lr.append(l_relay(1, lo[1]))
-    lr.append(l_relay(2, lo[2]))
+    choose_rows()
     uf_moves = [u_forward(0, uo[0])]
-    choose_rows()
     choose_ancestors(0, 4)
-    ls = [l_share(0, lr[0])]
-    choose_ancestors(4, 8)
-    zn = ring2(0, z_ring, zn)
     ls[0].wait_recv()
     chunk(1, 0, (0, 2))
-    ls.append(l_share(1, lr[1]))
+    zn = ring2(0, z_ring, zn)
+    chunk(1, 0, (2, 4))
     uf_moves.append(u_forward(1, uo[1]))
-    chunk(1, 0, (2, 4))
-    ls.append(l_share(2, lr[2]))
+    ls.append(l_share(1, lo[1]))
+    choose_ancestors(4, 8)
+    ls.append(l_share(2, lo[2]))
     uf_moves.append(u_forward(2, uo[2]))
+    local_u.wait()
     ls[1].wait_recv()
-    chunk(1, 1)
+    chunk(1, 1, (0, 2))
     ring3(0, z_ring, zn)
-    yn = ring1(0, y_ring)
+    yn = y_send(0)
+    chunk(1, 1, (2, 4))
     ls[2].wait_recv()
     chunk(1, 2)
     lower_term(1)
     zf = ring1(1, z_ring)
-    local_u.wait()
     for h in range(2):
         hs = pl.ds(h * 128, 128)
         hi, low = split(xi[h])
@@ -430,15 +424,16 @@
         c.wait_recv()
     upper_prep(0)
     upper_chunk(0)
-    yn = ring2(0, y_ring, yn)
+    y_sum(0, yn)
+    xn = x_swap(0)
     pivot_chunk(0)
     zf = ring2(1, z_ring, zf)
     for c in uf_moves[1]:
         c.wait_recv()
     upper_prep(1)
     upper_chunk(1)
-    ring3(0, y_ring, yn)
-    xn = x_swap(0)
+    x_add(0, xn)
+    exchange(0)
     pivot_chunk(1)
     for c in uf_moves[2]:
         c.wait_recv()
@@ -455,26 +450,24 @@
             pvs[g * 8 : g * 8 + 8, :] + mine * placed[(g % 8) * 8 : (g % 8) * 8 + 8, :]
         )
     p1 = send(pvb.at[1 - core], pc, d_core)
+    ring3(1, z_ring, zf)
+    yf = y_send(1)
     upper_chunk(2)
     for g in range(32):
         at = (g % 2, (g // 4) % 4, ((g // 2) % 2) * 2 + g // 16)
         cb[at[0], at[1], at[2]] = -y[g * 8 : g * 8 + 8, :]
     to_core = send(cb.at[1 - core], rc, d_core)
-    ring3(1, z_ring, zf)
-    yf = ring1(1, y_ring)
     p1.wait_recv()
     pvb[core] += pc[...]
 
-    def in_plane(n, other):
+    def in_plane(n):
         zz, xx = (z + n // 4) % 4, (x + n) % 4
-        cc = (core + other) % 2
-        return zz, xx, ((xx % 2) * 4 + zz, (xx // 2) * 2 + cc, col)
+        return zz, xx, ((xx % 2) * 4 + zz, (xx // 2) * 2 + core, col)
 
     p2 = []
     for n in range(1, 16):
-        zz, xx, dev = in_plane(n, 0)
+        zz, xx, dev = in_plane(n)
         p2.append(send(pvb.at[core, zz, xx], pz.at[n - 1], dev))
-    x_add(0, xn)
     to_core.wait_recv()
 
     @pl.loop(0, 4)
@@ -483,7 +476,8 @@
 
     f1p = send(cb.at[core, z2, pl.ds(0, 2)], ru1.at[0], d_zp)
     f1m = send(cb.at[core, z2, pl.ds(2, 2)], ru1.at[1], d_zm)
-    yf = ring2(1, y_ring, yf)
+    y_sum(1, yf)
+    xf = x_swap(1)
     for g in range(32):
         k = (g % 2) * 16 + ((g // 4) % 4) * 4 + ((g // 2) % 2) * 2 + g // 16
         bsp[k * 8 : k * 8 + 8, :] = bs_ref[g * 8 : g * 8 + 8, :]
@@ -491,8 +485,6 @@
         c.wait_recv()
     pb[col] = pvb[core, z, x] + jnp.sum(pz[...], 0)
     p4 = [send(pb.at[col], pb.at[col], at_y((col + d) % 4)) for d in range(1, 4)]
-    ring3(1, y_ring, yf)
-    xf = x_swap(1)
     f1p.wait_recv()
     cb[core, zp, 0:2] += ru1[0]
     f2p = send(cb.at[core, zp], ru2.at[0], d_zp)
@@ -503,45 +495,45 @@
         c.wait_recv()
     pfull[core, z, x] = pb[0] + pb[1] + pb[2] + pb[3]
     p5 = []
-    for n in range(1, 32):
-        zz, xx, dev = in_plane(n // 2, n % 2)
+    for n in range(1, 16):
+        zz, xx, dev = in_plane(n)
         p5.append(send(pfull.at[core, z, x], pfull.at[core, z, x], dev))
     x_add(1, xf)
-    exchange()
+    exchange(1)
     f2p.wait_recv()
     f2m.wait_recv()
     cb[core, z] += ru2[0] + ru2[1]
-    rest = T - LEFT
-    h1p = send(cb.at[core, z, x2, :, pl.ds(0, LEFT)], rv1.at[0], d_xp)
-    h1m = send(cb.at[core, z, x2, :, pl.ds(LEFT, rest)], rv1.at[1, :, pl.ds(0, rest)], d_xm)
-    h1p.wait_recv()
-    cb[core, z, xp, :, :LEFT] += rv1[0]
-    h2p = send(cb.at[core, z, xp], rv2.at[0], d_xp)
-    h1m.wait_recv()
-    cb[core, z, xm, :, LEFT:] += rv1[1, :, :rest]
-    h2m = send(cb.at[core, z, xm], rv2.at[1], d_xm)
+    h1 = [
+        send(cb.at[core, z, (x + d) % 4], rv.at[d - 1], at_x((x + d) % 4)) for d in range(1, 4)
+    ]
     for c in p5:
         c.wait_recv()
+    p6 = send(pfull.at[core], pfull.at[core], d_core)
+    for c in h1:
+        c.wait_recv()
+    out_ref[:, :T] = cb[core, z, x] + rv[0] + rv[1] + rv[2]
+    p6.wait_recv()
     pivot = pfull[...].reshape(S, S)
     charge = jnp.sum(bsp[...] * three(pivot, bs_ref[...]), 0, keepdims=True)
-
-    pltpu.make_async_copy(got.at[pl.ds(0, DEV - 1)], got.at[pl.ds(0, DEV - 1)], arecv.at[0]).wait()
-    received = got[...].reshape(8 * DEV, 128)
-    both = jnp.concatenate([bs_ref[0:128, :], bs_ref[128:256, :]], 1)
-    projected = three(received, both)
-    first = (iota((8 * DEV, 128), 0) // 4) % 2 == 0
-    projected = jnp.where(first, projected[:, :128], projected[:, 128:])
-    charge = charge + jnp.sum(ba8[...] * projected, 0, keepdims=True)
-    h2p.wait_recv()
-    h2m.wait_recv()
-    out_ref[:, :T] = cb[core, z, x] + rv2[0] + rv2[1]
+    others = pl.ds(0, DEV - 1)
+    for h in range(2):
+        pltpu.make_async_copy(got.at[h, others], got.at[h, others], arecv.at[h]).wait()
+    received = jnp.concatenate([got[h].reshape(4 * DEV, 128) for h in range(2)], 1)
+    projected = three(received, bs_ref[...])
+    charge = charge + jnp.sum(ba4[...] * projected, 0, keepdims=True)
     out_ref[:, T:] = jnp.broadcast_to(charge, (8, 128))
-    pltpu.make_async_copy(pk.at[pl.ds(0, DEV - 1)], pk.at[pl.ds(0, DEV - 1)], asend.at[0]).wait()
+    for n in range(2):
+        pltpu.make_async_copy(pk.at[n, others], pk.at[n, others], asend.at[n]).wait()
     for c in started:
         c.wait_send()
 
 
 N_COPIES = 112
+
+
+def hand_out(both_ref, upper_ref, charge_ref):
+    upper_ref[...] = both_ref[:, :T]
+    charge_ref[...] = both_ref[0:1, T:]
 
 
 def fused(weights, tile, lower, upper, pivot, owners, basis_super, basis_ancestor):
@@ -558,7 +550,6 @@
             pltpu.VMEM((2, T, T), BF16),
             pltpu.VMEM((4, 2, Q, T), F32),
             pltpu.VMEM((4, 2, Q, T), F32),
-            pltpu.VMEM((2, Q, T), F32),
             pltpu.VMEM((4, S, T), BF16),
             pltpu.VMEM((4, S, T), BF16),
             pltpu.VMEM((2, S, T), BF16),
@@ -573,16 +564,14 @@
             pltpu.VMEM((2, T, 128), F32),
             pltpu.VMEM((2, BLK, 128), F32),
             pltpu.VMEM((2, 2, BLK, 128), F32),
-            pltpu.VMEM((2, SUB, 128), F32),
-            pltpu.VMEM((2, 2, SUB, 128), F32),
+            pltpu.VMEM((2, 3, SUB, 128), F32),
             pltpu.VMEM((2, SUB, 128), F32),
             pltpu.VMEM((2, SUB, 128), F32),
             pltpu.VMEM((2, 4, 4, 8, T), F32),
             pltpu.VMEM((4, 4, 8, T), F32),
             pltpu.VMEM((2, 2, 8, T), F32),
             pltpu.VMEM((2, 4, 8, T), F32),
-            pltpu.VMEM((2, 8, LEFT), F32),
-            pltpu.VMEM((2, 8, T), F32),
+            pltpu.VMEM((3, 8, T), F32),
             pltpu.VMEM((2, 4, 4, 8, S), F32),
             pltpu.VMEM((4, 4, 8, S), F32),
             pltpu.VMEM((15, 8, S), F32),
@@ -590,10 +579,10 @@
             pltpu.VMEM((2, 4, 4, 8, S), F32),
             pltpu.VMEM((S, 128), F32),
             pltpu.VMEM((4608, 128), F32),
-            pltpu.VMEM((8 * DEV, 128), F32),
-            pltpu.VMEM((8 * DEV, 2 * SUB), BF16),
-            pltpu.VMEM((DEV, 8, 128), F32),
-            pltpu.VMEM((DEV, 8, 128), F32),
+            pltpu.VMEM((4 * DEV, 128), F32),
+            pltpu.VMEM((4 * DEV, SUB), BF16),
+            pltpu.VMEM((2, DEV, 4, 128), F32),
+            pltpu.VMEM((2, DEV, 4, 128), F32),
             pltpu.VMEM((BAT, TOPK, WIDE), jnp.int32),
             pltpu.VMEM((S, S), F32),
             pltpu.VMEM((T, S), BF16),
@@ -602,8 +591,8 @@
             pltpu.SemaphoreType.DMA((N_COPIES,)),
             pltpu.SemaphoreType.DMA((N_COPIES,)),
             pltpu.SemaphoreType.DMA((7,)),
-            pltpu.SemaphoreType.DMA((1,)),
-            pltpu.SemaphoreType.DMA((1,)),
+            pltpu.SemaphoreType.DMA((2,)),
+            pltpu.SemaphoreType.DMA((2,)),
         ],
         compiler_params=pltpu.CompilerParams(
             collective_id=0, has_side_effects=True, vmem_limit_bytes=63 << 20
@@ -619,7 +608,11 @@
         pole_weights, inverse_tile, lower_factor, upper_factor, pivot_inverse, block_owners.T,
         basis_super, basis_ancestor,
     )
-    return (out[:, :T], out[0, T:])
+    upper_density, charge = pl.pallas_call(
+        hand_out,
+        out_shape=(jax.ShapeDtypeStruct((8, T), F32), jax.ShapeDtypeStruct((1, 128), F32)),
+    )(out)
+    return (upper_density, charge.reshape(128))
 
 
 def solution(mesh):

time: 68.9 us -> 64 us (0.929)
  local copies, waits for them, and re-layouts: 2.57 us -> 0 us
  Pallas kernels: 65.5 us -> 63.2 us
    pallas_call x1, Pallas kernels: 65.5 us -> 61.8 us  [fused(): pl.pallas_call(kernel, out_shape=jax.ShapeDtypeStruct((8, T + 128), F32),...]
    pallas_call x0 -> x1, Pallas kernels: none -> 1.4 us  [body(): pl.pallas_call(hand_out, out_shape=(jax.ShapeDtypeStruct((8, T), F32), ja...]
    slice x1 -> x0, local copies, waits for them, and re-layouts: 1.39 us -> none  [body(): return (out[:, :T], out[0, T:])]
    squeeze x1 -> x0, local copies, waits for them, and re-layouts: 1.19 us -> none  [body(): return (out[:, :T], out[0, T:])]
where the time goes in v4:
time: 64 us; the launch traced here: 63.8 us
  Pallas kernels  63.2 us (99%)
  between operations  0.64 us (1%)
    pallas_call x1, Pallas kernels, fused(): pl.pallas_call(kernel, out_shape=jax.ShapeDtypeStruct((8, T + 128), F32),...  61.8 us
    pallas_call x1, Pallas kernels, body(): pl.pallas_call(hand_out, out_shape=(jax.ShapeDtypeStruct((8, T), F32), ja...  1.4 us

profile of v4, /device:TPU:0, one launch (start us, length us, event | category | flops | bytes accessed | tf_op | source)
XLA Modules:
  0.0 63.8 jit_solution(8976935968566968524)
XLA Ops:
  0.6 61.8 %shard_map.95.both_ref = f32[8,1280]{1,0:T(8,128)} custom-call(f32[1,2]{1,0:T(1,128)} %w_ref.1, f32[1,2,1152,1152]{3,2,1,0:T(8,128)} %a_hbm.1, f32[1,2,64,1152]{3,2,1,0:T(8,128)} %l_hbm.1, f32[1,2,64,1152]{3,2,1,0:T(8,128)} %u_hbm.1, f32[1,2,64,64]{3,2,1,0:T(8,128)} %piv_ref.1, s32[6,2304]{1,0:T(8,128)} %bitcast.2, f32[256,128]{1,0:T(8,128)} %bs_ref.1, ...), custom_call_target="tpu_custom_call" | custom-call | tf_op jit(solution)/shard_map/pallas_call | solution.py:542
  62.4 1.4 %shard_map.96 = (f32[8,1152]{1,0:T(8,128)}, f32[1,128]{1,0:T(1,128)}) custom-call(f32[8,1280]{1,0:T(8,128)} %shard_map.95.both_ref), custom_call_target="tpu_custom_call" | custom-call | tf_op jit(solution)/shard_map/pallas_call | solution.py:611

commit v5 on v4

--- a/solution.py
+++ b/solution.py
@@ -20,6 +20,7 @@
 BLK = 288
 SUB = 72
 TAIL = 1024
+LEFT = 640
 
 
 def nt(a, b):
@@ -51,7 +52,7 @@
     w_ref, a_hbm, l_hbm, u_hbm, piv_ref, own_ref, bs_ref, ba_hbm,
     out_ref,
     a32, ah, al, lf, uf, bl, br, uph, upl, xr, xi, xih, xil, xrh, xrl, y, lt,
-    rz1, rz2, ry, rx, ld, cb, rc, ru1, ru2, rv,
+    rz1, rz2, ry, rx, ld, cb, rc, ra, rb, rv,
     pvb, pc, pz, pb, pfull, bsp, ba, ba4, sel, pk, got, own_s, pvs, ath, atl, bt,
     sends, recvs, locs, asend, arecv,
 ):
@@ -261,14 +262,13 @@
                 uph[part, rs, lane] = hi
                 upl[part, rs, lane] = low
 
-    def upper_chunk(k):
+    def upper_chunk(k, parts=(0, 1)):
         lane = lanes(k)
-        acc = nn(uph[0, :, lane], ah[1, lane, :])
-        acc = acc + nn(uph[0, :, lane], al[1, lane, :])
-        acc = acc + nn(upl[0, :, lane], ah[1, lane, :])
-        acc = acc + nn(uph[1, :, lane], ah[0, lane, :])
-        acc = acc + nn(uph[1, :, lane], al[0, lane, :])
-        acc = acc + nn(upl[1, :, lane], ah[0, lane, :])
+        acc = None
+        for part in parts:
+            for left, right in ((uph, ah), (uph, al), (upl, ah)):
+                one = nn(left[part, :, lane], right[1 - part, lane, :])
+                acc = one if acc is None else acc + one
         if k == 0:
             y[...] = acc
         else:
@@ -393,23 +393,21 @@
     lower_term(0)
     zn = ring1(0, z_ring)
     choose_rows()
+    choose_ancestors(0, 4)
     uf_moves = [u_forward(0, uo[0])]
-    choose_ancestors(0, 4)
     ls[0].wait_recv()
-    chunk(1, 0, (0, 2))
+    chunk(1, 0)
     zn = ring2(0, z_ring, zn)
-    chunk(1, 0, (2, 4))
-    uf_moves.append(u_forward(1, uo[1]))
     ls.append(l_share(1, lo[1]))
     choose_ancestors(4, 8)
     ls.append(l_share(2, lo[2]))
+    uf_moves.append(u_forward(1, uo[1]))
     uf_moves.append(u_forward(2, uo[2]))
     local_u.wait()
     ls[1].wait_recv()
-    chunk(1, 1, (0, 2))
+    chunk(1, 1)
     ring3(0, z_ring, zn)
     yn = y_send(0)
-    chunk(1, 1, (2, 4))
     ls[2].wait_recv()
     chunk(1, 2)
     lower_term(1)
@@ -431,9 +429,6 @@
     for c in uf_moves[1]:
         c.wait_recv()
     upper_prep(1)
-    upper_chunk(1)
-    x_add(0, xn)
-    exchange(0)
     pivot_chunk(1)
     for c in uf_moves[2]:
         c.wait_recv()
@@ -450,6 +445,20 @@
             pvs[g * 8 : g * 8 + 8, :] + mine * placed[(g % 8) * 8 : (g % 8) * 8 + 8, :]
         )
     p1 = send(pvb.at[1 - core], pc, d_core)
+    x_add(0, xn)
+    exchange(0)
+    p1.wait_recv()
+    pvb[core] += pc[...]
+
+    def in_plane(n):
+        zz, xx = (z + n // 4) % 4, (x + n) % 4
+        return zz, xx, ((xx % 2) * 4 + zz, (xx // 2) * 2 + core, col)
+
+    p2 = []
+    for n in range(1, 16):
+        zz, xx, dev = in_plane(n)
+        p2.append(send(pvb.at[core, zz, xx], pz.at[n - 1], dev))
+    upper_chunk(1)
     ring3(1, z_ring, zf)
     yf = y_send(1)
     upper_chunk(2)
@@ -457,40 +466,31 @@
         at = (g % 2, (g // 4) % 4, ((g // 2) % 2) * 2 + g // 16)
         cb[at[0], at[1], at[2]] = -y[g * 8 : g * 8 + 8, :]
     to_core = send(cb.at[1 - core], rc, d_core)
-    p1.wait_recv()
-    pvb[core] += pc[...]
-
-    def in_plane(n):
-        zz, xx = (z + n // 4) % 4, (x + n) % 4
-        return zz, xx, ((xx % 2) * 4 + zz, (xx // 2) * 2 + core, col)
-
-    p2 = []
-    for n in range(1, 16):
-        zz, xx, dev = in_plane(n)
-        p2.append(send(pvb.at[core, zz, xx], pz.at[n - 1], dev))
+    for c in p2:
+        c.wait_recv()
+    pb[col] = pvb[core, z, x] + jnp.sum(pz[...], 0)
+    p4 = [send(pb.at[col], pb.at[col], at_y((col + d) % 4)) for d in range(1, 4)]
+    for g in range(32):
+        k = (g % 2) * 16 + ((g // 4) % 4) * 4 + ((g // 2) % 2) * 2 + g // 16
+        bsp[k * 8 : k * 8 + 8, :] = bs_ref[g * 8 : g * 8 + 8, :]
     to_core.wait_recv()
 
     @pl.loop(0, 4)
     def _(b):
         cb[core, b] += rc[b]
 
-    f1p = send(cb.at[core, z2, pl.ds(0, 2)], ru1.at[0], d_zp)
-    f1m = send(cb.at[core, z2, pl.ds(2, 2)], ru1.at[1], d_zm)
     y_sum(1, yf)
     xf = x_swap(1)
-    for g in range(32):
-        k = (g % 2) * 16 + ((g // 4) % 4) * 4 + ((g // 2) % 2) * 2 + g // 16
-        bsp[k * 8 : k * 8 + 8, :] = bs_ref[g * 8 : g * 8 + 8, :]
-    for c in p2:
-        c.wait_recv()
-    pb[col] = pvb[core, z, x] + jnp.sum(pz[...], 0)
-    p4 = [send(pb.at[col], pb.at[col], at_y((col + d) % 4)) for d in range(1, 4)]
-    f1p.wait_recv()
-    cb[core, zp, 0:2] += ru1[0]
-    f2p = send(cb.at[core, zp], ru2.at[0], d_zp)
-    f1m.wait_recv()
-    cb[core, zm, 2:4] += ru1[1]
-    f2m = send(cb.at[core, zm], ru2.at[1], d_zm)
+
+    wide, rest = pl.ds(0, LEFT), pl.ds(LEFT, T - LEFT)
+    fa = [
+        send(cb.at[core, (z + d) % 4, :, :, wide], ra.at[d - 1], at_z((z + d) % 4))
+        for d in range(1, 4)
+    ]
+    fb = [
+        send(cb.at[core, :, (x + d) % 4, :, rest], rb.at[d - 1], at_x((x + d) % 4))
+        for d in range(1, 4)
+    ]
     for c in p4:
         c.wait_recv()
     pfull[core, z, x] = pb[0] + pb[1] + pb[2] + pb[3]
@@ -500,16 +500,24 @@
         p5.append(send(pfull.at[core, z, x], pfull.at[core, z, x], dev))
     x_add(1, xf)
     exchange(1)
-    f2p.wait_recv()
-    f2m.wait_recv()
-    cb[core, z] += ru2[0] + ru2[1]
-    h1 = [
-        send(cb.at[core, z, (x + d) % 4], rv.at[d - 1], at_x((x + d) % 4)) for d in range(1, 4)
+    for c in fb:
+        c.wait_recv()
+    cb[core, :, x, :, LEFT:] += rb[0] + rb[1] + rb[2]
+    hb = [
+        send(cb.at[core, (z + d) % 4, x, :, rest], rv.at[d - 1, :, rest], at_z((z + d) % 4))
+        for d in range(1, 4)
+    ]
+    for c in fa:
+        c.wait_recv()
+    cb[core, z, :, :, :LEFT] += ra[0] + ra[1] + ra[2]
+    ha = [
+        send(cb.at[core, z, (x + d) % 4, :, wide], rv.at[d - 1, :, wide], at_x((x + d) % 4))
+        for d in range(1, 4)
     ]
     for c in p5:
         c.wait_recv()
     p6 = send(pfull.at[core], pfull.at[core], d_core)
-    for c in h1:
+    for c in hb + ha:
         c.wait_recv()
     out_ref[:, :T] = cb[core, z, x] + rv[0] + rv[1] + rv[2]
     p6.wait_recv()
@@ -569,8 +577,8 @@
             pltpu.VMEM((2, SUB, 128), F32),
             pltpu.VMEM((2, 4, 4, 8, T), F32),
             pltpu.VMEM((4, 4, 8, T), F32),
-            pltpu.VMEM((2, 2, 8, T), F32),
-            pltpu.VMEM((2, 4, 8, T), F32),
+            pltpu.VMEM((3, 4, 8, LEFT), F32),
+            pltpu.VMEM((3, 4, 8, T - LEFT), F32),
             pltpu.VMEM((3, 8, T), F32),
             pltpu.VMEM((2, 4, 4, 8, S), F32),
             pltpu.VMEM((4, 4, 8, S), F32),

time: 64 us -> 64.2 us (level); the launches traced: 63.8 us -> 63.1 us
  Pallas kernels: 63.2 us -> 62.4 us
    pallas_call x1, Pallas kernels: 61.8 us -> 61 us  [fused(): pl.pallas_call(kernel, out_shape=jax.ShapeDtypeStruct((8, T + 128), F32),...]
where the time goes in v5:
time: 64.2 us; the launch traced here: 63.1 us
  Pallas kernels  62.4 us (97%)
    pallas_call x1, Pallas kernels, fused(): pl.pallas_call(kernel, out_shape=jax.ShapeDtypeStruct((8, T + 128), F32),...  61 us
    pallas_call x1, Pallas kernels, body(): pl.pallas_call(hand_out, out_shape=(jax.ShapeDtypeStruct((8, T), F32), ja...  1.4 us

profile of v5, /device:TPU:0, one launch (start us, length us, event | category | flops | bytes accessed | tf_op | source)
XLA Modules:
  0.0 63.1 jit_solution(6534325463885106097)
XLA Ops:
  0.6 61.0 %shard_map.95.both_ref = f32[8,1280]{1,0:T(8,128)} custom-call(f32[1,2]{1,0:T(1,128)} %w_ref.1, f32[1,2,1152,1152]{3,2,1,0:T(8,128)} %a_hbm.1, f32[1,2,64,1152]{3,2,1,0:T(8,128)} %l_hbm.1, f32[1,2,64,1152]{3,2,1,0:T(8,128)} %u_hbm.1, f32[1,2,64,64]{3,2,1,0:T(8,128)} %piv_ref.1, s32[6,2304]{1,0:T(8,128)} %bitcast.2, f32[256,128]{1,0:T(8,128)} %bs_ref.1, ...), custom_call_target="tpu_custom_call" | custom-call | tf_op jit(solution)/shard_map/pallas_call | solution.py:550
  61.7 1.4 %shard_map.96 = (f32[8,1152]{1,0:T(8,128)}, f32[1,128]{1,0:T(1,128)}) custom-call(f32[8,1280]{1,0:T(8,128)} %shard_map.95.both_ref), custom_call_target="tpu_custom_call" | custom-call | tf_op jit(solution)/shard_map/pallas_call | solution.py:619

commit v6 on v5

--- a/solution.py
+++ b/solution.py
@@ -401,11 +401,11 @@
     ls.append(l_share(1, lo[1]))
     choose_ancestors(4, 8)
     ls.append(l_share(2, lo[2]))
-    uf_moves.append(u_forward(1, uo[1]))
-    uf_moves.append(u_forward(2, uo[2]))
     local_u.wait()
     ls[1].wait_recv()
     chunk(1, 1)
+    uf_moves.append(u_forward(1, uo[1]))
+    uf_moves.append(u_forward(2, uo[2]))
     ring3(0, z_ring, zn)
     yn = y_send(0)
     ls[2].wait_recv()

time: 64.2 us -> 66.3 us (1.033); the launches traced: 63.1 us -> 65.8 us
  Pallas kernels: 62.4 us -> 65.2 us
    pallas_call x1, Pallas kernels: 61 us -> 63.8 us  [fused(): pl.pallas_call(kernel, out_shape=jax.ShapeDtypeStruct((8, T + 128), F32),...]
where the time goes in v6:
time: 66.3 us; the launch traced here: 65.8 us
  Pallas kernels  65.2 us (98%)
    pallas_call x1, Pallas kernels, fused(): pl.pallas_call(kernel, out_shape=jax.ShapeDtypeStruct((8, T + 128), F32),...  63.8 us
    pallas_call x1, Pallas kernels, body(): pl.pallas_call(hand_out, out_shape=(jax.ShapeDtypeStruct((8, T), F32), ja...  1.4 us

profile of v6, /device:TPU:0, one launch (start us, length us, event | category | flops | bytes accessed | tf_op | source)
XLA Modules:
  0.0 65.8 jit_solution(5612897068291179755)
XLA Ops:
  0.6 63.8 %shard_map.95.both_ref = f32[8,1280]{1,0:T(8,128)} custom-call(f32[1,2]{1,0:T(1,128)} %w_ref.1, f32[1,2,1152,1152]{3,2,1,0:T(8,128)} %a_hbm.1, f32[1,2,64,1152]{3,2,1,0:T(8,128)} %l_hbm.1, f32[1,2,64,1152]{3,2,1,0:T(8,128)} %u_hbm.1, f32[1,2,64,64]{3,2,1,0:T(8,128)} %piv_ref.1, s32[6,2304]{1,0:T(8,128)} %bitcast.2, f32[256,128]{1,0:T(8,128)} %bs_ref.1, ...), custom_call_target="tpu_custom_call" | custom-call | tf_op jit(solution)/shard_map/pallas_call | solution.py:550
  64.4 1.4 %shard_map.96 = (f32[8,1152]{1,0:T(8,128)}, f32[1,128]{1,0:T(1,128)}) custom-call(f32[8,1280]{1,0:T(8,128)} %shard_map.95.both_ref), custom_call_target="tpu_custom_call" | custom-call | tf_op jit(solution)/shard_map/pallas_call | solution.py:619

commit v7 on v5

--- a/solution.py
+++ b/solution.py
@@ -262,13 +262,14 @@
                 uph[part, rs, lane] = hi
                 upl[part, rs, lane] = low
 
-    def upper_chunk(k, parts=(0, 1)):
+    def upper_chunk(k):
         lane = lanes(k)
-        acc = None
-        for part in parts:
-            for left, right in ((uph, ah), (uph, al), (upl, ah)):
-                one = nn(left[part, :, lane], right[1 - part, lane, :])
-                acc = one if acc is None else acc + one
+        acc = nn(uph[0, :, lane], ah[1, lane, :])
+        acc = acc + nn(uph[0, :, lane], al[1, lane, :])
+        acc = acc + nn(upl[0, :, lane], ah[1, lane, :])
+        acc = acc + nn(uph[1, :, lane], ah[0, lane, :])
+        acc = acc + nn(uph[1, :, lane], al[0, lane, :])
+        acc = acc + nn(upl[1, :, lane], ah[0, lane, :])
         if k == 0:
             y[...] = acc
         else:
@@ -393,21 +394,23 @@
     lower_term(0)
     zn = ring1(0, z_ring)
     choose_rows()
+    uf_moves = [u_forward(0, uo[0])]
     choose_ancestors(0, 4)
-    uf_moves = [u_forward(0, uo[0])]
     ls[0].wait_recv()
-    chunk(1, 0)
+    chunk(1, 0, (0, 2))
     zn = ring2(0, z_ring, zn)
+    chunk(1, 0, (2, 4))
+    uf_moves.append(u_forward(1, uo[1]))
     ls.append(l_share(1, lo[1]))
     choose_ancestors(4, 8)
     ls.append(l_share(2, lo[2]))
-    uf_moves.append(u_forward(1, uo[1]))
     uf_moves.append(u_forward(2, uo[2]))
     local_u.wait()
     ls[1].wait_recv()
-    chunk(1, 1)
+    chunk(1, 1, (0, 2))
     ring3(0, z_ring, zn)
     yn = y_send(0)
+    chunk(1, 1, (2, 4))
     ls[2].wait_recv()
     chunk(1, 2)
     lower_term(1)

time: 64.2 us -> 64.8 us (level); the launches traced: 63.1 us -> 64.6 us
  Pallas kernels: 62.4 us -> 64 us
    pallas_call x1, Pallas kernels: 61 us -> 62.6 us  [fused(): pl.pallas_call(kernel, out_shape=jax.ShapeDtypeStruct((8, T + 128), F32),...]
where the time goes in v7:
time: 64.8 us; the launch traced here: 64.6 us
  Pallas kernels  64 us (99%)
    pallas_call x1, Pallas kernels, fused(): pl.pallas_call(kernel, out_shape=jax.ShapeDtypeStruct((8, T + 128), F32),...  62.6 us
    pallas_call x1, Pallas kernels, body(): pl.pallas_call(hand_out, out_shape=(jax.ShapeDtypeStruct((8, T), F32), ja...  1.4 us

profile of v7, /device:TPU:0, one launch (start us, length us, event | category | flops | bytes accessed | tf_op | source)
XLA Modules:
  0.0 64.6 jit_solution(4381988623695475717)
XLA Ops:
  0.6 62.6 %shard_map.95.both_ref = f32[8,1280]{1,0:T(8,128)} custom-call(f32[1,2]{1,0:T(1,128)} %w_ref.1, f32[1,2,1152,1152]{3,2,1,0:T(8,128)} %a_hbm.1, f32[1,2,64,1152]{3,2,1,0:T(8,128)} %l_hbm.1, f32[1,2,64,1152]{3,2,1,0:T(8,128)} %u_hbm.1, f32[1,2,64,64]{3,2,1,0:T(8,128)} %piv_ref.1, s32[6,2304]{1,0:T(8,128)} %bitcast.2, f32[256,128]{1,0:T(8,128)} %bs_ref.1, ...), custom_call_target="tpu_custom_call" | custom-call | tf_op jit(solution)/shard_map/pallas_call | solution.py:553
  63.2 1.4 %shard_map.96 = (f32[8,1152]{1,0:T(8,128)}, f32[1,128]{1,0:T(1,128)}) custom-call(f32[8,1280]{1,0:T(8,128)} %shard_map.95.both_ref), custom_call_target="tpu_custom_call" | custom-call | tf_op jit(solution)/shard_map/pallas_call | solution.py:622
